TPU v7x, 256 devices: a whole 4x4x8 slice. The times are simulated.
256 devices in a mesh: atoms: 32 (over z, y_hi, core), kvec: 8 (over y_lo, x).
Axes of the slice: x: 4, y: 4 (y_hi: 2, y_lo: 2; y = y_hi * 2 + y_lo), z: 8, core: 2. Of those that a mesh axis runs over, the one named last changes fastest.
Arguments:
- particle_traits: bfloat16 [131072, 256], P('atoms'), may hold values from -6 to 6
- particle_coordinates: float32 [3, 131072], P(None, 'atoms'), may hold values from 0 to 24
- kspace_vectors: float32 [3, 4096], P(None, 'kvec'), may hold values from -1.5 to 1.5
- learned_kspace_filter: float32 [4096, 256], P('kvec'), may hold values from -4 to 4
- spatial_home: int32 [32, 4096], P('atoms'), may hold values from 0 to 4095, each once within a row
- following_halo_lines: int32 [32, 512], P('atoms'), may hold values from 0 to 4095
- previous_halo_lines: int32 [32, 512], P('atoms'), may hold values from 0 to 4095
- sender_projection: bfloat16 [256, 256], replicated, may hold values from -0.375 to 0.375
- receiver_projection: bfloat16 [256, 256], replicated, may hold values from -0.375 to 0.375
- pair_channel_mapping: bfloat16 [196, 256], replicated, may hold values from -0.375 to 0.375
- vertex_rescaling_gain: float32 [256], replicated, may hold values from 0.1 to 1.9
- link_sender_line: int32 [1048576], P(('atoms', 'kvec')), may hold values from 0 to 5119
- link_receiver_particle: int32 [1048576], P(('atoms', 'kvec')), may hold values from 0 to 4095
- active_link_tally: int32 [256], P(('atoms', 'kvec')), may hold values from 32 to 4096, as said below
Outputs:
- orbital_blocks: bfloat16 [196, 1048576], P(None, ('atoms', 'kvec'))
- partitioned: bfloat16 [131072, 256], P('atoms')
Inputs may be any that keep to these rules, and one draw needn't show every extreme that they name: `spatial_home`: each row of destination orders one device's 4096 atoms; every device sends exactly 128 atoms to every partition. `following_halo_lines`: rows of the sending partition. `previous_halo_lines`: rows of the sending partition. `link_sender_line`: A table row: the partition's 4096 own atoms, then 512 ghosts from the previous partition, then 512 from the next. `active_link_tally`: A multiple of 32; the used edges are the first ones of a device's list; some device uses all 4096 slots.
All inputs are finite; a program needn't handle non-finite values.
Results may differ from a plain program's by a relative error of at most 0.01.
Values may be sent and summed in bfloat16 or wider, within the bound.
No kernel may reach another device: no remote copies, remote signals or barrier semaphores. Data moves between devices by JAX's collectives and lax.ppermute only.
A program may use at most 64 MiB of HBM per device.

v0:
```python
import functools
import math

import jax
import jax.numpy as jnp
from jax import lax
from jax.experimental import pallas as pl
from jax.experimental.pallas import tpu as pltpu
from jax.sharding import Mesh
from jax.sharding import PartitionSpec as P

BF = jnp.bfloat16
F32 = jnp.float32
ATOM_AXES = ("z", "yh", "core")
PLANE_AXES = ("z", "yh")
KV_AXES = ("yl", "x")
TILE = 512
TRIG_ROWS = 16

SIN_TERMS = (
    4.442882919124345,
    -7.30824568650903,
    3.6063542184324517,
    -0.8461116503720991,
    0.10982451642340209,
)
COS_TERMS = (
    1.4142134962552282,
    -6.978850948563795,
    5.739460376906981,
    -1.8835579059858576,
    0.31068802752541236,
)


def cos_sin_of_turns(turns):
    r = turns - jnp.round(turns)
    z = r * r
    u = SIN_TERMS[4] * z + SIN_TERMS[3]
    v = COS_TERMS[4] * z + COS_TERMS[3]
    for term in (2, 1, 0):
        u = u * z + SIN_TERMS[term]
        v = v * z + COS_TERMS[term]
    u = u * r
    return 1.0 - u * u, u * v


def three_parts(values):
    first = values.astype(BF).astype(F32)
    rest = values - first
    second = rest.astype(BF).astype(F32)
    third = (rest - second).astype(BF).astype(F32)
    return first, second, third


def store_atom_parts(parts_ref, coordinates):
    a, b, c = three_parts(coordinates)
    for place, part in enumerate((a, a, a, b, b, c)):
        parts_ref[3 * place : 3 * place + 3, :] = part


def store_kspace_parts(parts_ref, vectors):
    a, b, c = three_parts(vectors * (0.5 / math.pi))
    for place, part in enumerate((a, b, c, a, b, a)):
        parts_ref[3 * place : 3 * place + 3, :] = part


def struct_kernel(coord_ref, kvec_ref, feat_ref, out_ref, apart, kpart, klhs, phase, cosv, sinv, acc):
    step = pl.program_id(0)
    kdev = kvec_ref.shape[1]

    @pl.when(step == 0)
    def _():
        apart[...] = jnp.zeros_like(apart)
        kpart[...] = jnp.zeros_like(kpart)
        store_kspace_parts(kpart, kvec_ref[...])
        klhs[...] = kpart[...].T.astype(BF)
        acc[...] = jnp.zeros_like(acc)

    store_atom_parts(apart, coord_ref[...])
    phase[...] = jnp.dot(klhs[...], apart[...].astype(BF), preferred_element_type=F32)

    def some_rows(i, carry):
        rows = pl.ds(pl.multiple_of(i * TRIG_ROWS, TRIG_ROWS), TRIG_ROWS)
        c, s = cos_sin_of_turns(phase[rows, :])
        cosv[rows, :] = c.astype(BF)
        sinv[rows, :] = s.astype(BF)
        return carry

    lax.fori_loop(0, kdev // TRIG_ROWS, some_rows, 0, unroll=4)
    acc[0] += jnp.dot(cosv[...], feat_ref[...], preferred_element_type=F32)
    acc[1] += jnp.dot(sinv[...], feat_ref[...], preferred_element_type=F32)

    @pl.when(step == pl.num_programs(0) - 1)
    def _():
        pieces = out_ref.shape[0]
        piece = out_ref.shape[2]
        for part in range(2):
            out_ref[:, part] = acc[part].reshape(pieces, piece, -1).astype(BF)


def struct_call(coordinates, vectors, feats, pieces):
    atoms, chans = feats.shape
    kdev = vectors.shape[1]
    return pl.pallas_call(
        struct_kernel,
        out_shape=jax.ShapeDtypeStruct((pieces, 2, kdev // pieces, chans), BF),
        grid=(atoms // TILE,),
        in_specs=[
            pl.BlockSpec((3, TILE), lambda i: (0, i)),
            pl.BlockSpec((3, kdev), lambda i: (0, 0)),
            pl.BlockSpec((TILE, chans), lambda i: (i, 0)),
        ],
        out_specs=pl.BlockSpec((pieces, 2, kdev // pieces, chans), lambda i: (0, 0, 0, 0)),
        scratch_shapes=[
            pltpu.VMEM((128, TILE), F32),
            pltpu.VMEM((128, kdev), F32),
            pltpu.VMEM((kdev, 128), BF),
            pltpu.VMEM((kdev, TILE), F32),
            pltpu.VMEM((kdev, TILE), BF),
            pltpu.VMEM((kdev, TILE), BF),
            pltpu.VMEM((2, kdev, chans), F32),
        ],
        cost_estimate=pl.CostEstimate(flops=6 * atoms * kdev * chans, transcendentals=0, bytes_accessed=4 << 20),
        name="struct",
    )(coordinates, vectors, feats)


def waves_kernel(place_ref, coord_ref, kvec_ref, want_ref, feat_ref, waves_ref, picked_ref, apart, kpart, krhs, rows, ordered, phase, acc):
    step = pl.program_id(0)
    atoms = coord_ref.shape[1]
    kdev = kvec_ref.shape[1]

    @pl.when(step == 0)
    def _():
        apart[...] = jnp.zeros_like(apart)
        kpart[...] = jnp.zeros_like(kpart)
        store_kspace_parts(kpart, kvec_ref[...])
        krhs[...] = kpart[...].astype(BF)
        acc[...] = jnp.zeros_like(acc)
        for part in range(atoms // TILE):
            span = slice(part * TILE, (part + 1) * TILE)
            store_atom_parts(apart, coord_ref[:, span])
            rows[span, :] = apart[...].T

        def move(i, carry):
            base = i * 16
            for j in range(16):
                ordered[pl.ds(place_ref[base + j], 1), :] = rows[pl.ds(base + j, 1), :]
            return carry

        lax.fori_loop(0, atoms // 16, move, 0)

    here = pl.ds(pl.multiple_of(step * TILE, TILE), TILE)
    phase[...] = jnp.dot(ordered[here, :].astype(BF), krhs[...], preferred_element_type=F32)

    def some_rows(i, carry):
        span = pl.ds(pl.multiple_of(i * TRIG_ROWS, TRIG_ROWS), TRIG_ROWS)
        c, s = cos_sin_of_turns(phase[span, :])
        waves_ref[span, :kdev] = c.astype(BF)
        waves_ref[span, kdev:] = s.astype(BF)
        return carry

    lax.fori_loop(0, TILE // TRIG_ROWS, some_rows, 0, unroll=4)

    wanted = acc.shape[0]
    hot = lax.broadcasted_iota(jnp.int32, (wanted, TILE), 0) == want_ref[...]
    acc[...] += jnp.dot(
        jnp.where(hot, 1.0, 0.0).astype(BF), feat_ref[...], preferred_element_type=F32
    )

    @pl.when(step == pl.num_programs(0) - 1)
    def _():
        picked_ref[...] = acc[...].astype(BF)


def waves_call(places, want, coordinates, vectors, feats, wanted):
    atoms, chans = feats.shape
    kdev = vectors.shape[1]
    return pl.pallas_call(
        waves_kernel,
        out_shape=(
            jax.ShapeDtypeStruct((atoms, 2 * kdev), BF),
            jax.ShapeDtypeStruct((wanted, chans), BF),
        ),
        grid_spec=pltpu.PrefetchScalarGridSpec(
            num_scalar_prefetch=1,
            grid=(atoms // TILE,),
            in_specs=[
                pl.BlockSpec((3, atoms), lambda i, p: (0, 0)),
                pl.BlockSpec((3, kdev), lambda i, p: (0, 0)),
                pl.BlockSpec((1, TILE), lambda i, p: (0, i)),
                pl.BlockSpec((TILE, chans), lambda i, p: (i, 0)),
            ],
            out_specs=(
                pl.BlockSpec((TILE, 2 * kdev), lambda i, p: (i, 0)),
                pl.BlockSpec((wanted, chans), lambda i, p: (0, 0)),
            ),
            scratch_shapes=[
                pltpu.VMEM((128, TILE), F32),
                pltpu.VMEM((128, kdev), F32),
                pltpu.VMEM((128, kdev), BF),
                pltpu.VMEM((atoms, 128), F32),
                pltpu.VMEM((atoms, 128), F32),
                pltpu.VMEM((TILE, kdev), F32),
                pltpu.VMEM((wanted, chans), F32),
            ],
        ),
        cost_estimate=pl.CostEstimate(flops=4 * atoms * kdev * chans, transcendentals=0, bytes_accessed=12 << 20),
        name="waves",
    )(places, coordinates, vectors, want, feats)


def update_kernel(waves_ref, filt_ref, out_ref, filt):
    kdev = filt.shape[0] // 2

    @pl.when(pl.program_id(0) == 0)
    def _():
        for part in range(2):
            filt[part * kdev : (part + 1) * kdev, :] = filt_ref[:, part].reshape(kdev, -1)

    out_ref[...] = jnp.dot(waves_ref[...], filt[...], preferred_element_type=F32).astype(BF)


def update_call(waves, filtered):
    atoms, columns = waves.shape
    chans = filtered.shape[-1]
    return pl.pallas_call(
        update_kernel,
        out_shape=jax.ShapeDtypeStruct((atoms, chans), BF),
        grid=(atoms // TILE,),
        in_specs=[
            pl.BlockSpec((TILE, columns), lambda i: (i, 0)),
            pl.BlockSpec(filtered.shape, lambda i: (0, 0, 0, 0)),
        ],
        out_specs=pl.BlockSpec((TILE, chans), lambda i: (i, 0)),
        scratch_shapes=[pltpu.VMEM((columns, chans), BF)],
        cost_estimate=pl.CostEstimate(flops=2 * atoms * columns * chans, transcendentals=0, bytes_accessed=11 << 20),
        name="update",
    )(waves, filtered)


def node_kernel(parts_ref, feat_ref, gain_ref, out_ref):
    update = parts_ref[0].astype(F32)
    for part in range(1, parts_ref.shape[0]):
        update = update + parts_ref[part].astype(F32)
    refreshed = feat_ref[...].astype(F32) + update / (1.0 + jnp.exp(-update))
    mean = jnp.mean(refreshed * refreshed, axis=-1, keepdims=True)
    out_ref[...] = (refreshed * lax.rsqrt(mean + 1e-06) * gain_ref[...]).astype(BF)


def node_call(parts, feats, gain):
    count, rows, chans = parts.shape
    block = 128
    return pl.pallas_call(
        node_kernel,
        out_shape=jax.ShapeDtypeStruct((rows, chans), BF),
        grid=(rows // block,),
        in_specs=[
            pl.BlockSpec((count, block, chans), lambda i: (0, i, 0)),
            pl.BlockSpec((block, chans), lambda i: (i, 0)),
            pl.BlockSpec((1, chans), lambda i: (0, 0)),
        ],
        out_specs=pl.BlockSpec((block, chans), lambda i: (i, 0)),
        cost_estimate=pl.CostEstimate(flops=20 * rows * chans, transcendentals=rows * chans, bytes_accessed=3 << 20),
        name="node",
    )(parts, feats, gain)


def relay_kernel(rows_ref, ids_ref, out_ref, halo_ref, acc):
    step = pl.program_id(0)
    here = jnp.swapaxes(rows_ref[...], 0, 1).reshape(out_ref.shape)
    out_ref[...] = here
    tile = out_ref.shape[0]
    hot = lax.broadcasted_iota(jnp.int32, (1, tile), 1) == ids_ref[...] - step * tile
    got = jnp.dot(jnp.where(hot, 1.0, 0.0).astype(BF), here, preferred_element_type=F32)

    @pl.when(step == 0)
    def _():
        acc[...] = got

    @pl.when(step > 0)
    def _():
        acc[...] += got

    @pl.when(step == pl.num_programs(0) - 1)
    def _():
        halo_ref[...] = acc[...].astype(BF)


def relay_call(rows, ids):
    groups, sources, per, chans = rows.shape
    tiles = 8
    halo = ids.shape[0]
    atoms = groups * sources * per
    return pl.pallas_call(
        relay_kernel,
        out_shape=(
            jax.ShapeDtypeStruct((atoms, chans), BF),
            jax.ShapeDtypeStruct((halo, chans), BF),
        ),
        grid=(tiles,),
        in_specs=[
            pl.BlockSpec((groups, sources // tiles, per, chans), lambda i: (0, i, 0, 0)),
            pl.BlockSpec((halo, 1), lambda i: (0, 0)),
        ],
        out_specs=(
            pl.BlockSpec((atoms // tiles, chans), lambda i: (i, 0)),
            pl.BlockSpec((halo, chans), lambda i: (0, 0)),
        ),
        scratch_shapes=[pltpu.VMEM((halo, chans), F32)],
        cost_estimate=pl.CostEstimate(flops=2 * halo * atoms * chans, transcendentals=0, bytes_accessed=5 << 20),
        name="relay",
    )(rows, ids)


def edges_kernel(src_ref, dst_ref, count_ref, own_ref, lower_ref, upper_ref, wl_ref, wr_ref, map_ref, out_ref, left, right, pair):
    step = pl.program_id(0)
    atoms = own_ref.shape[0]
    ghosts = lower_ref.shape[0]

    def project(rows, weight_ref, table, at):
        count = rows.shape[0]
        got = jnp.dot(rows, weight_ref[...], preferred_element_type=F32).astype(BF).astype(F32)
        for half in range(2):
            table[pl.ds(2 * at + half, count, stride=2), :] = got[:, half * 128 : half * 128 + 128]

    @pl.when(step == 0)
    def _():
        for part in range(atoms // TILE):
            rows = own_ref[part * TILE : (part + 1) * TILE, :]
            project(rows, wl_ref, left, part * TILE)
            project(rows, wr_ref, right, part * TILE)
        project(lower_ref[...], wl_ref, left, atoms)
        project(upper_ref[...], wl_ref, left, atoms + ghosts)

    block = out_ref.shape[1]

    def some_edges(i, carry):
        base = i * 16
        for j in range(16):
            at = step * block + base + j
            a = left[pl.ds(pl.multiple_of(src_ref[at] * 2, 2), 2), :]
            b = right[pl.ds(pl.multiple_of(dst_ref[at] * 2, 2), 2), :]
            pair[pl.ds(pl.multiple_of((base + j) * 2, 2), 2), :] = a * b
        return carry

    lax.fori_loop(0, block // 16, some_edges, 0)
    total = None
    for half in range(2):
        value = pair[pl.ds(half, block, stride=2), :].astype(BF)
        part = lax.dot_general(
            map_ref[:, half * 128 : half * 128 + 128],
            value,
            (((1,), (1,)), ((), ())),
            preferred_element_type=F32,
        )
        total = part if total is None else total + part
    at = step * block + lax.broadcasted_iota(jnp.int32, (1, block), 1)
    out_ref[...] = jnp.where(at < count_ref[0], total, 0.0).astype(BF)


def edges_call(src, dst, count, own, lower, upper, wl, wr, mapping):
    atoms, chans = own.shape
    ghosts = lower.shape[0]
    edges = src.shape[0]
    orb = mapping.shape[0]
    whole = lambda a: pl.BlockSpec(a.shape, lambda i, *_: (0, 0))
    return pl.pallas_call(
        edges_kernel,
        out_shape=jax.ShapeDtypeStruct((orb, edges), BF),
        grid_spec=pltpu.PrefetchScalarGridSpec(
            num_scalar_prefetch=3,
            grid=(edges // TILE,),
            in_specs=[whole(a) for a in (own, lower, upper, wl, wr, mapping)],
            out_specs=pl.BlockSpec((orb, TILE), lambda i, *_: (0, i)),
            scratch_shapes=[
                pltpu.VMEM((2 * (atoms + 2 * ghosts), 128), F32),
                pltpu.VMEM((2 * atoms, 128), F32),
                pltpu.VMEM((2 * TILE, 128), F32),
            ],
        ),
        cost_estimate=pl.CostEstimate(flops=2 * edges * chans * orb, transcendentals=0, bytes_accessed=8 << 20),
        name="edges",
    )(src, dst, count, own, lower, upper, wl, wr, mapping)


def exchange(pieces, axes):
    return lax.all_to_all(pieces, axes, 0, 0, tiled=True)


def gather_over(piece, axes):
    copies = lax.axis_size(axes)
    return exchange(jnp.broadcast_to(piece[None], (copies,) + piece.shape), axes)


def local(
    particle_traits,
    particle_coordinates,
    kspace_vectors,
    learned_kspace_filter,
    spatial_home,
    following_halo_lines,
    previous_halo_lines,
    sender_projection,
    receiver_projection,
    pair_channel_mapping,
    vertex_rescaling_gain,
    link_sender_line,
    link_receiver_particle,
    active_link_tally,
):
    n_atoms = lax.axis_size(ATOM_AXES)
    n_planes = lax.axis_size(PLANE_AXES)
    n_cores = lax.axis_size("core")
    n_kvec = lax.axis_size(KV_AXES)
    atoms, chans = particle_traits.shape
    kdev = kspace_vectors.shape[1]
    norm_scale = 1.0 / math.sqrt(atoms * n_atoms * kdev * n_kvec)
    share = atoms // n_kvec
    run = atoms // n_atoms // n_kvec
    piece = kdev // n_atoms

    partial = struct_call(particle_coordinates, kspace_vectors, particle_traits, n_atoms)
    partial = partial.reshape(n_cores, n_planes, 2, piece, chans)
    halves = exchange(partial, "core")
    chip = jnp.sum(halves.astype(F32), axis=0).astype(BF)
    spread = exchange(chip, PLANE_AXES)

    home = spatial_home[0]
    places = (home // run % n_kvec) * share + home // (run * n_kvec) * run + home % run
    want = (places - lax.axis_index(KV_AXES) * share)[None, :]
    waves, feats = waves_call(
        places, want, particle_coordinates, kspace_vectors, particle_traits, share
    )

    struct = jnp.sum(spread.astype(F32), axis=0)
    at = (lax.axis_index("core") * n_planes + lax.axis_index(PLANE_AXES)) * piece
    filter_piece = lax.dynamic_slice_in_dim(learned_kspace_filter, at, piece, 0)
    filtered = (filter_piece[None] * struct * norm_scale).astype(BF)
    filtered = gather_over(filtered, PLANE_AXES)
    filtered = lax.all_gather(filtered, "core", axis=0, tiled=True)

    update = update_call(waves, filtered)
    parts = exchange(update.reshape(n_kvec, share, chans), KV_AXES)
    node = node_call(parts, feats, vertex_rescaling_gain[None, :])
    arrived = exchange(node.reshape(n_atoms, run, chans), ATOM_AXES)
    everything = gather_over(arrived, KV_AXES)
    ids = jnp.concatenate([following_halo_lines[0], previous_halo_lines[0]])[:, None]
    partition_rows, halo = relay_call(everything.reshape(n_kvec, n_atoms, run, chans), ids)
    ghosts = following_halo_lines.shape[1]
    up = [(i, (i + 1) % n_atoms) for i in range(n_atoms)]
    down = [(i, (i - 1) % n_atoms) for i in range(n_atoms)]
    lower = lax.ppermute(halo[:ghosts], ATOM_AXES, up)
    upper = lax.ppermute(halo[ghosts:], ATOM_AXES, down)
    orbital_blocks = edges_call(
        link_sender_line,
        link_receiver_particle,
        active_link_tally,
        partition_rows,
        lower,
        upper,
        sender_projection,
        receiver_projection,
        pair_channel_mapping,
    )
    return (orbital_blocks, partition_rows)


def solution(mesh):
    fine = Mesh(mesh.devices.reshape(8, 2, 2, 2, 4), ATOM_AXES + KV_AXES)
    every = ATOM_AXES + KV_AXES
    placed = (
        P(ATOM_AXES, None),
        P(None, ATOM_AXES),
        P(None, KV_AXES),
        P(KV_AXES, None),
        P(ATOM_AXES, None),
        P(ATOM_AXES, None),
        P(ATOM_AXES, None),
        P(),
        P(),
        P(),
        P(),
        P(every),
        P(every),
        P(every),
    )
    return jax.shard_map(
        local,
        mesh=fine,
        in_specs=placed,
        out_specs=(P(None, every), P(ATOM_AXES, None)),
        check_vma=False,
    )
```

profile of v0, /device:TPU:7, one launch (start us, length us, event | category | flops | bytes accessed | tf_op | source)
XLA Modules:
  0.0 216.4 jit_solution(1848251123550866580)
XLA Ops:
  0.6 15.1 %struct.1 = bf16[32,2,16,256]{3,2,1,0:T(8,128)(2,1)} custom-call(f32[3,4096]{1,0:T(4,128)} %coord_ref.3, f32[3,512]{1,0:T(4,128)} %kvec_ref.3, bf16[4096,256]{1,0:T(8,128)(2,1)} %feat_ref.3), custom_call_target="tpu_custom_call" | custom-call | flops 3221225472 | bytes 4194304 | tf_op jit(solution)/shard_map/struct/pallas_call | solution.py:105
  15.8 5.6 %all_to_all.30 = bf16[2,16,2,16,256]{4,3,2,1,0:T(8,128)(2,1)S(1)} all-to-all(bf16[2,16,2,16,256]{4,3,2,1,0:T(8,128)(2,1)} %bitcast.10), channel_id=1, replica_groups=mesh['z'=8,'yh'=2,'core'=2,'yl'=2,'x'=4] {'core'}, dimensions={0} | all-to-all | bytes 1048576 | tf_op jit(solution)/shard_map/all_to_all | solution.py:389
  21.4 0.8 reduce_sum.21
  22.2 11.0 %all-to-all-start.1 = ((bf16[16,2,16,256]{3,2,1,0:T(8,128)(2,1)}), bf16[16,2,16,256]{3,2,1,0:T(8,128)(2,1)S(1)}, u32[]{:S(2)}, u32[]{:S(2)}) async-start(bf16[16,2,16,256]{3,2,1,0:T(8,128)(2,1)} %reduce_sum.21), calls=%async_computation.1 | async-start | bytes 524288 | tf_op jit(solution)/shard_map/all_to_all | solution.py:389
  33.2 12.5 %all-to-all-done.1 = bf16[16,2,16,256]{3,2,1,0:T(8,128)(2,1)S(1)} async-done(((bf16[16,2,16,256]{3,2,1,0:T(8,128)(2,1)}), bf16[16,2,16,256]{3,2,1,0:T(8,128)(2,1)S(1)}, u32[]{:S(2)}, u32[]{:S(2)}) %all-to-all-start.1) | async-done | bytes 262176 | tf_op jit(solution)/shard_map/all_to_all | solution.py:389
  46.5 3.5 %all-to-all-start.2 = ((bf16[16,2,16,256]{3,2,1,0:T(8,128)(2,1)}), bf16[16,2,16,256]{3,2,1,0:T(8,128)(2,1)S(1)}, u32[]{:S(2)}, u32[]{:S(2)}) async-start(bf16[16,2,16,256]{3,2,1,0:T(8,128)(2,1)} %broadcast_in_dim.8), calls=%async_computation.2 | async-start | bytes 524288 | tf_op jit(solution)/shard_map/all_to_all | solution.py:389
  50.0 0.8 fusion.10.want_ref
  51.5 19.7 %waves.1 = (bf16[4096,1024]{1,0:T(8,128)(2,1)}, bf16[512,256]{1,0:T(8,128)(2,1)}) custom-call(s32[4096]{0:T(1024)} %fusion.4.place_ref, f32[3,4096]{1,0:T(4,128)} %coord_ref.3, f32[3,512]{1,0:T(4,128)} %kvec_ref.3, s32[1,4096]{1,0:T(1,128)} %fusion.10.want_ref, bf16[4096,256]{1,0:T(8,128)(2,1)} %feat_ref.3), custom_call_target="tpu_custom_call" | custom-call | flops 2147483648 | bytes 12582912 | tf_op jit(solution)/shard_map/waves/pallas_call | solution.py:180
  71.2 3.9 %all_gather.3.filt_ref = bf16[32,2,16,256]{3,2,1,0:T(8,128)(2,1)} all-gather(bf16[16,2,16,256]{3,2,1,0:T(8,128)(2,1)S(1)} %all-to-all-done.2), channel_id=1, replica_groups=mesh['z'=8,'yh'=2,'core'=2,'yl'=2,'x'=4] {'core'}, dimensions={0}, use_global_device_ids=true | all-gather | bytes 786432 | tf_op jit(solution)/shard_map/all_gather | solution.py:442
  75.1 8.7 %update.1 = bf16[4096,256]{1,0:T(8,128)(2,1)} custom-call(bf16[4096,1024]{1,0:T(8,128)(2,1)} %get-tuple-element.6.waves_ref, bf16[32,2,16,256]{3,2,1,0:T(8,128)(2,1)} %all_gather.3.filt_ref), custom_call_target="tpu_custom_call" | custom-call | flops 2147483648 | bytes 11534336 | tf_op jit(solution)/shard_map/update/pallas_call | solution.py:228
  83.8 28.5 %all_to_all.31.parts_ref = bf16[8,512,256]{2,1,0:T(8,128)(2,1)} all-to-all(bf16[8,512,256]{2,1,0:T(8,128)(2,1)} %bitcast.8), channel_id=1, replica_groups=mesh['z'=8,'yh'=2,'core'=2,'yl'=2,'x'=4] {'yl','x'}, dimensions={0} | all-to-all | bytes 4194304 | tf_op jit(solution)/shard_map/all_to_all | solution.py:389
  112.3 3.8 %node.1 = bf16[512,256]{1,0:T(8,128)(2,1)} custom-call(bf16[8,512,256]{2,1,0:T(8,128)(2,1)} %all_to_all.31.parts_ref, bf16[512,256]{1,0:T(8,128)(2,1)} %get-tuple-element.7.feat_ref, f32[1,256]{1,0:T(1,128)} %bitcast.15), custom_call_target="tpu_custom_call" | custom-call | flops 2621440 | bytes 3145728 | tf_op jit(solution)/shard_map/node/pallas_call | solution.py:255
  116.1 25.1 %all_to_all.32 = bf16[32,16,256]{2,1,0:T(8,128)(2,1)S(1)} all-to-all(bf16[32,16,256]{2,1,0:T(8,128)(2,1)} %bitcast.9), channel_id=1, replica_groups=mesh['z'=8,'yh'=2,'core'=2,'yl'=2,'x'=4] {'z','yh','core'}, dimensions={0} | all-to-all | bytes 524288 | tf_op jit(solution)/shard_map/all_to_all | solution.py:389
  141.2 1.5 broadcast_in_dim.10
  142.7 5.5 %all-to-all-start.5 = ((bf16[8,32,16,256]{3,2,1,0:T(8,128)(2,1)}), bf16[8,32,16,256]{3,2,1,0:T(8,128)(2,1)S(1)}, u32[]{:S(2)}, u32[]{:S(2)}) async-start(bf16[8,32,16,256]{3,2,1,0:T(8,128)(2,1)} %broadcast_in_dim.10), calls=%async_computation.5 | async-start | bytes 4194304 | tf_op jit(solution)/shard_map/all_to_all | solution.py:389
  148.2 1.0 copy.18.ids_ref
  149.3 28.6 %all-to-all-done.5.rows_ref = bf16[8,32,16,256]{3,2,1,0:T(8,128)(2,1)S(1)} async-done(((bf16[8,32,16,256]{3,2,1,0:T(8,128)(2,1)}), bf16[8,32,16,256]{3,2,1,0:T(8,128)(2,1)S(1)}, u32[]{:S(2)}, u32[]{:S(2)}) %all-to-all-start.5) | async-done | bytes 2097184 | tf_op jit(solution)/shard_map/all_to_all | solution.py:389
  177.8 1.3 copy-done.1
  179.2 8.2 %relay.1 = (bf16[4096,256]{1,0:T(8,128)(2,1)}, bf16[1024,256]{1,0:T(8,128)(2,1)}) custom-call(bf16[8,32,16,256]{3,2,1,0:T(8,128)(2,1)} %copy-done.1, s32[1024,1]{1,0:T(8,128)} %copy.18.ids_ref), custom_call_target="tpu_custom_call" | custom-call | flops 2147483648 | bytes 5242880 | tf_op jit(solution)/shard_map/relay/pallas_call | solution.py:296
  187.4 1.1 fusion.15
  188.5 1.4 collective-permute-start.1
  190.6 4.1 %collective-permute-done.lower_ref = bf16[512,256]{1,0:T(8,128)(2,1)S(1)} collective-permute-done((bf16[512,256]{1,0:T(8,128)(2,1)S(1)}, bf16[512,256]{1,0:T(8,128)(2,1)S(1)}, u32[]{:S(2)}, u32[]{:S(2)}) %collective-permute-start) | collective-permute-done | bytes 262176 | tf_op jit(solution)/shard_map/ppermute | solution.py:454
  194.6 4.2 %collective-permute-done.1.upper_ref = bf16[512,256]{1,0:T(8,128)(2,1)S(1)} collective-permute-done((bf16[512,256]{1,0:T(8,128)(2,1)S(1)}, bf16[512,256]{1,0:T(8,128)(2,1)S(1)}, u32[]{:S(2)}, u32[]{:S(2)}) %collective-permute-start.1) | collective-permute-done | bytes 262176 | tf_op jit(solution)/shard_map/ppermute | solution.py:455
  199.6 16.8 %edges.1 = bf16[196,4096]{1,0:T(8,128)(2,1)} custom-call(s32[4096]{0:T(1024)} %src_ref.1, s32[4096]{0:T(1024)} %dst_ref.1, s32[1]{0:T(128)S(6)} %copy.19.count_ref, bf16[4096,256]{1,0:T(8,128)(2,1)} %get-tuple-element.5.own_ref, bf16[512,256]{1,0:T(8,128)(2,1)} %copy-done.2, bf16[512,256]{1,0:T(8,128)(2,1)} %copy-done.3, bf16[256,256]{1,0:T(8,128)(2,1)} %wl_ref.1, ...), custom_call_target="tpu_custom_call" | custom-call | flops 411041792 | bytes 8388608 | tf_op jit(solution)/shard_map/edges/pallas_call | solution.py:369
  (21 shorter events, 2.3 us)
Async XLA Ops:
  0.6 32.6 %copy-start = (f32[512,256]{1,0:T(8,128)S(1)}, f32[512,256]{1,0:T(8,128)}, u32[]{:S(2)}) copy-start(f32[512,256]{1,0:T(8,128)} %param.17) | copy-start | bytes 1572868
  15.8 34.3 %copy-start.4 = (s32[1,4096]{1,0:T(1,128)S(1)}, s32[1,4096]{1,0:T(1,128)}, u32[]{:S(2)}) copy-start(s32[1,4096]{1,0:T(1,128)} %param.18) | copy-start | bytes 49156
  22.2 23.5 %all-to-all-start.1 = ((bf16[16,2,16,256]{3,2,1,0:T(8,128)(2,1)}), bf16[16,2,16,256]{3,2,1,0:T(8,128)(2,1)S(1)}, u32[]{:S(2)}, u32[]{:S(2)}) async-start(bf16[16,2,16,256]{3,2,1,0:T(8,128)(2,1)} %reduce_sum.21), calls=%async_computation.1 | async-start | bytes 524288 | tf_op jit(solution)/shard_map/all_to_all | solution.py:389
  46.5 24.7 %all-to-all-start.2 = ((bf16[16,2,16,256]{3,2,1,0:T(8,128)(2,1)}), bf16[16,2,16,256]{3,2,1,0:T(8,128)(2,1)S(1)}, u32[]{:S(2)}, u32[]{:S(2)}) async-start(bf16[16,2,16,256]{3,2,1,0:T(8,128)(2,1)} %broadcast_in_dim.8), calls=%async_computation.2 | async-start | bytes 524288 | tf_op jit(solution)/shard_map/all_to_all | solution.py:389
  142.7 5.5 %copy-start.5 = (s32[1,512]{1,0:T(1,128)S(1)}, s32[1,512]{1,0:T(1,128)}, u32[]{:S(2)}) copy-start(s32[1,512]{1,0:T(1,128)} %param.20) | copy-start | bytes 6148
  142.7 5.5 %copy-start.6 = (s32[1,512]{1,0:T(1,128)S(1)}, s32[1,512]{1,0:T(1,128)}, u32[]{:S(2)}) copy-start(s32[1,512]{1,0:T(1,128)} %param.19) | copy-start | bytes 6148
  142.7 35.1 %all-to-all-start.5 = ((bf16[8,32,16,256]{3,2,1,0:T(8,128)(2,1)}), bf16[8,32,16,256]{3,2,1,0:T(8,128)(2,1)S(1)}, u32[]{:S(2)}, u32[]{:S(2)}) async-start(bf16[8,32,16,256]{3,2,1,0:T(8,128)(2,1)} %broadcast_in_dim.10), calls=%async_computation.5 | async-start | bytes 4194304 | tf_op jit(solution)/shard_map/all_to_all | solution.py:389
  177.8 1.3 copy-start.1
  188.4 6.2 %collective-permute-start = (bf16[512,256]{1,0:T(8,128)(2,1)S(1)}, bf16[512,256]{1,0:T(8,128)(2,1)S(1)}, u32[]{:S(2)}, u32[]{:S(2)}) collective-permute-start(bf16[512,256]{1,0:T(8,128)(2,1)S(1)} %get-tuple-element.11), channel_id=1, source_target_pairs={{0,8},{8,16},{16,24},{24,32},{32,40},{40,48},{48,56},{56,64},{64,7... | collective-permute-start | bytes 786440 | tf_op jit(solution)/shard_map/ppermute | solution.py:454
  188.5 10.4 %collective-permute-start.1 = (bf16[512,256]{1,0:T(8,128)(2,1)S(1)}, bf16[512,256]{1,0:T(8,128)(2,1)S(1)}, u32[]{:S(2)}, u32[]{:S(2)}) collective-permute-start(bf16[512,256]{1,0:T(8,128)(2,1)S(1)} %get-tuple-element.10), channel_id=1, source_target_pairs={{0,248},{8,0},{16,8},{24,16},{32,24},{40,32},{48,40},{56,48},{64,5... | collective-permute-start | bytes 786440 | tf_op jit(solution)/shard_map/ppermute | solution.py:455
  194.6 4.2 %copy-start.2 = (bf16[512,256]{1,0:T(8,128)(2,1)}, bf16[512,256]{1,0:T(8,128)(2,1)S(1)}, u32[]{:S(2)}) copy-start(bf16[512,256]{1,0:T(8,128)(2,1)S(1)} %collective-permute-done.lower_ref) | copy-start | bytes 786436
  198.9 0.7 copy-start.3
where the time goes:
time: 218 us; the launch traced here: 216 us
  Pallas kernels  72.3 us (33%)
  blocking collectives  63.1 us (29%)
  waiting for transfers between devices  49.4 us (23%)
  starting transfers between devices  21.5 us (10%)
  local copies, waits for them, and re-layouts  6.39 us (3%)
  other arithmetic  2.37 us (1%)
    all_to_all x3, blocking collectives, exchange(): return lax.all_to_all(pieces, axes, 0, 0, tiled=True)  59.2 us
    all_to_all x3, waiting for transfers between devices, exchange(): return lax.all_to_all(pieces, axes, 0, 0, tiled=True)  41.1 us
    all_to_all x3, starting transfers between devices, exchange(): return lax.all_to_all(pieces, axes, 0, 0, tiled=True)  20 us
    pallas_call x1, Pallas kernels, waves_call(): pl.pallas_call(waves_kernel, out_shape=(jax.ShapeDtypeStruct((atoms, 2 *...  19.7 us
    pallas_call x1, Pallas kernels, edges_call(): pl.pallas_call(edges_kernel, out_shape=jax.ShapeDtypeStruct((orb, edges),...  16.8 us
    pallas_call x1, Pallas kernels, struct_call(): pl.pallas_call(struct_kernel, out_shape=jax.ShapeDtypeStruct((pieces, 2,...  15.1 us
    pallas_call x1, Pallas kernels, update_call(): pl.pallas_call(update_kernel, out_shape=jax.ShapeDtypeStruct((atoms, chan...  8.68 us
    pallas_call x1, Pallas kernels, relay_call(): pl.pallas_call(relay_kernel, out_shape=(jax.ShapeDtypeStruct((atoms, chan...  8.19 us
  transfers between devices with their start and end apart: 5, of which 4 were waited for; matrix products, arithmetic and copies ran while one was open for 1% of the time, Pallas kernels for 9%

commit v1 on v0

v1 whole, which is shorter than its diff:
```python
import functools
import math

import jax
import jax.numpy as jnp
from jax import lax
from jax.experimental import pallas as pl
from jax.experimental.pallas import tpu as pltpu
from jax.sharding import Mesh
from jax.sharding import PartitionSpec as P


BF = jnp.bfloat16
F32 = jnp.float32
ATOM_AXES = ("z", "yh", "core")
PLANE_AXES = ("z", "yh")
KV_AXES = ("yl", "x")
TILE = 512
TRIG_ROWS = 16

SIN_TERMS = (
    4.442882919124345,
    -7.30824568650903,
    3.6063542184324517,
    -0.8461116503720991,
    0.10982451642340209,
)
COS_TERMS = (
    1.4142134962552282,
    -6.978850948563795,
    5.739460376906981,
    -1.8835579059858576,
    0.31068802752541236,
)


def cos_sin_of_turns(turns):
    r = turns - jnp.round(turns)
    z = r * r
    u = SIN_TERMS[4] * z + SIN_TERMS[3]
    v = COS_TERMS[4] * z + COS_TERMS[3]
    for term in (2, 1, 0):
        u = u * z + SIN_TERMS[term]
        v = v * z + COS_TERMS[term]
    u = u * r
    return 1.0 - u * u, u * v


def three_parts(values):
    first = values.astype(BF).astype(F32)
    rest = values - first
    second = rest.astype(BF).astype(F32)
    third = (rest - second).astype(BF).astype(F32)
    return first, second, third


def store_atom_parts(parts_ref, coordinates):
    a, b, c = three_parts(coordinates)
    for place, part in enumerate((a, a, a, b, b, c)):
        parts_ref[3 * place : 3 * place + 3, :] = part


def store_kspace_parts(parts_ref, vectors):
    a, b, c = three_parts(vectors * (0.5 / math.pi))
    for place, part in enumerate((a, b, c, a, b, a)):
        parts_ref[3 * place : 3 * place + 3, :] = part


def own_first(vectors, core):
    half = vectors.shape[1] // 2
    a, b = vectors[:, :half], vectors[:, half:]
    first = core == 0
    return jnp.concatenate([jnp.where(first, a, b), jnp.where(first, b, a)], axis=1)


def params(megabytes):
    return pltpu.CompilerParams(vmem_limit_bytes=megabytes << 20)


def struct_kernel(core_ref, coord_ref, kvec_ref, feat_ref, keep_ref, send_ref, apart, kpart, klhs, phase, cosv, sinv, acc):
    step = pl.program_id(0)
    kdev = kvec_ref.shape[1]

    @pl.when(step == 0)
    def _():
        apart[...] = jnp.zeros_like(apart)
        kpart[...] = jnp.zeros_like(kpart)
        store_kspace_parts(kpart, own_first(kvec_ref[...], core_ref[0]))
        klhs[...] = kpart[...].T.astype(BF)
        acc[...] = jnp.zeros_like(acc)

    store_atom_parts(apart, coord_ref[...])
    phase[...] = jnp.dot(klhs[...], apart[...].astype(BF), preferred_element_type=F32)

    def some_rows(i, carry):
        rows = pl.ds(pl.multiple_of(i * TRIG_ROWS, TRIG_ROWS), TRIG_ROWS)
        c, s = cos_sin_of_turns(phase[rows, :])
        cosv[rows, :] = c.astype(BF)
        sinv[rows, :] = s.astype(BF)
        return carry

    lax.fori_loop(0, kdev // TRIG_ROWS, some_rows, 0, unroll=4)
    acc[0] += jnp.dot(cosv[...], feat_ref[...], preferred_element_type=F32)
    acc[1] += jnp.dot(sinv[...], feat_ref[...], preferred_element_type=F32)

    @pl.when(step == pl.num_programs(0) - 1)
    def _():
        planes, _, piece, chans = keep_ref.shape
        half = kdev // 2
        for part in range(2):
            keep_ref[:, part] = acc[part, :half].reshape(planes, piece, chans).astype(BF)
            send_ref[:, part] = acc[part, half:].reshape(planes, piece, chans).astype(BF)


def struct_call(core, coordinates, vectors, feats, planes):
    atoms, chans = feats.shape
    kdev = vectors.shape[1]
    shape = (planes, 2, kdev // 2 // planes, chans)
    return pl.pallas_call(
        struct_kernel,
        out_shape=[jax.ShapeDtypeStruct(shape, BF)] * 2,
        grid_spec=pltpu.PrefetchScalarGridSpec(
            num_scalar_prefetch=1,
            grid=(atoms // TILE,),
            in_specs=[
                pl.BlockSpec((3, TILE), lambda i, c: (0, i)),
                pl.BlockSpec((3, kdev), lambda i, c: (0, 0)),
                pl.BlockSpec((TILE, chans), lambda i, c: (i, 0)),
            ],
            out_specs=[pl.BlockSpec(shape, lambda i, c: (0, 0, 0, 0))] * 2,
            scratch_shapes=[
                pltpu.VMEM((128, TILE), F32),
                pltpu.VMEM((128, kdev), F32),
                pltpu.VMEM((kdev, 128), BF),
                pltpu.VMEM((kdev, TILE), F32),
                pltpu.VMEM((kdev, TILE), BF),
                pltpu.VMEM((kdev, TILE), BF),
                pltpu.VMEM((2, kdev, chans), F32),
            ],
        ),
        compiler_params=params(16),
        cost_estimate=pl.CostEstimate(flops=6 * atoms * kdev * chans, transcendentals=0, bytes_accessed=4 << 20),
        name="struct",
    )(core, coordinates, vectors, feats)


def order_kernel(place_ref, core_ref, coord_ref, kvec_ref, want_ref, feat_ref, ordered_ref, krhs_ref, picked_ref, apart, kpart, rows, ordered, acc):
    atoms = coord_ref.shape[1]
    wanted = picked_ref.shape[0]
    apart[...] = jnp.zeros_like(apart)
    kpart[...] = jnp.zeros_like(kpart)
    store_kspace_parts(kpart, own_first(kvec_ref[...], core_ref[0]))
    krhs_ref[...] = kpart[...].astype(BF)
    for part in range(atoms // TILE):
        span = slice(part * TILE, (part + 1) * TILE)
        store_atom_parts(apart, coord_ref[:, span])
        rows[span, :] = apart[...].T

    def move(i, carry):
        base = i * 32
        for j in range(32):
            ordered[pl.ds(place_ref[base + j], 1), :] = rows[pl.ds(base + j, 1), :]
        return carry

    lax.fori_loop(0, atoms // 32, move, 0)
    acc[...] = jnp.zeros_like(acc)

    def pick(i, carry):
        span = pl.ds(pl.multiple_of(i * TILE, TILE), TILE)
        ordered_ref[span, :] = ordered[span, :].astype(BF)
        hot = lax.broadcasted_iota(jnp.int32, (wanted, TILE), 0) == want_ref[:, span]
        acc[...] += jnp.dot(
            jnp.where(hot, 1.0, 0.0).astype(BF), feat_ref[span, :], preferred_element_type=F32
        )
        return carry

    lax.fori_loop(0, atoms // TILE, pick, 0)
    picked_ref[...] = acc[...].astype(BF)


def order_call(places, want, core, coordinates, vectors, feats, wanted):
    atoms, chans = feats.shape
    kdev = vectors.shape[1]
    whole = pl.BlockSpec(memory_space=pltpu.VMEM)
    return pl.pallas_call(
        order_kernel,
        out_shape=(
            jax.ShapeDtypeStruct((atoms, 128), BF),
            jax.ShapeDtypeStruct((128, kdev), BF),
            jax.ShapeDtypeStruct((wanted, chans), BF),
        ),
        grid_spec=pltpu.PrefetchScalarGridSpec(
            num_scalar_prefetch=2,
            grid=(),
            in_specs=[whole] * 4,
            out_specs=(whole,) * 3,
            scratch_shapes=[
                pltpu.VMEM((128, TILE), F32),
                pltpu.VMEM((128, kdev), F32),
                pltpu.VMEM((atoms, 128), F32),
                pltpu.VMEM((atoms, 128), F32),
                pltpu.VMEM((wanted, chans), F32),
            ],
        ),
        compiler_params=params(16),
        cost_estimate=pl.CostEstimate(flops=4 * atoms * kdev * chans, transcendentals=0, bytes_accessed=12 << 20),
        name="order",
    )(places, core, coordinates, vectors, want, feats)


def update_kernel(rows_ref, krhs_ref, own_ref, other_ref, out_ref, phase, cosv, sinv):
    kdev = krhs_ref.shape[1]
    half = kdev // 2
    phase[...] = jnp.dot(rows_ref[...], krhs_ref[...], preferred_element_type=F32)

    def some_rows(i, carry):
        span = pl.ds(pl.multiple_of(i * TRIG_ROWS, TRIG_ROWS), TRIG_ROWS)
        c, s = cos_sin_of_turns(phase[span, :])
        cosv[span, :] = c.astype(BF)
        sinv[span, :] = s.astype(BF)
        return carry

    lax.fori_loop(0, rows_ref.shape[0] // TRIG_ROWS, some_rows, 0, unroll=4)
    total = None
    for part, wave in enumerate((cosv, sinv)):
        for place, ref in enumerate((own_ref, other_ref)):
            weights = ref[:, part].reshape(half, -1)
            got = jnp.dot(wave[:, place * half : (place + 1) * half], weights, preferred_element_type=F32)
            total = got if total is None else total + got
    out_ref[...] = total.astype(BF)


def update_call(tile, ordered, krhs, own, other):
    kdev = krhs.shape[1]
    chans = own.shape[-1]
    whole = lambda a: pl.BlockSpec(a.shape, lambda i: (0,) * a.ndim)
    return pl.pallas_call(
        update_kernel,
        out_shape=jax.ShapeDtypeStruct((TILE, chans), BF),
        grid=(1,),
        in_specs=[pl.BlockSpec((TILE, 128), lambda i: (tile, 0)), whole(krhs), whole(own), whole(other)],
        out_specs=pl.BlockSpec((TILE, chans), lambda i: (0, 0)),
        scratch_shapes=[
            pltpu.VMEM((TILE, kdev), F32),
            pltpu.VMEM((TILE, kdev), BF),
            pltpu.VMEM((TILE, kdev), BF),
        ],
        compiler_params=params(12),
        cost_estimate=pl.CostEstimate(flops=4 * TILE * kdev * chans, transcendentals=0, bytes_accessed=1 << 20),
        name="update",
    )(ordered, krhs, own, other)


def node_kernel(*refs):
    *part_refs, feat_ref, gain_ref, out_ref = refs
    update = part_refs[0][...].astype(F32)
    for ref in part_refs[1:]:
        update = update + ref[...].astype(F32)
    refreshed = feat_ref[...].astype(F32) + update / (1.0 + jnp.exp(-update))
    mean = jnp.mean(refreshed * refreshed, axis=-1, keepdims=True)
    out_ref[...] = (refreshed * lax.rsqrt(mean + 1e-06) * gain_ref[...]).astype(BF)


def node_call(parts, feats, gain):
    rows, chans = feats.shape
    block = 256
    tile = pl.BlockSpec((block, chans), lambda i: (i, 0))
    return pl.pallas_call(
        node_kernel,
        out_shape=jax.ShapeDtypeStruct((rows, chans), BF),
        grid=(rows // block,),
        in_specs=[tile] * (len(parts) + 1) + [pl.BlockSpec((1, chans), lambda i: (0, 0))],
        out_specs=tile,
        compiler_params=params(8),
        cost_estimate=pl.CostEstimate(flops=20 * rows * chans, transcendentals=rows * chans, bytes_accessed=3 << 20),
        name="node",
    )(*parts, feats, gain)


def pairs_of(piece_refs):
    for kv, refs in enumerate(piece_refs):
        at = 0
        for ref in refs:
            yield kv, at, ref
            at += ref.shape[0]


def store_rows(table, value, starts, run):
    for place, start in enumerate(starts):
        for half in range(2):
            table[pl.ds(start + half, run, stride=2), :] = value[
                place * run : (place + 1) * run, half * 128 : half * 128 + 128
            ]


def project_pieces(piece_refs, kv_ref, weight_ref, table, spots):
    for kv, at, ref in pairs_of(piece_refs):
        count, run, chans = ref.shape
        rows = ref[...].reshape(count * run, chans)
        got = jnp.dot(rows, weight_ref[...], preferred_element_type=F32).astype(BF).astype(F32)
        base = pl.multiple_of(kv_ref[kv] * (2 * run), 2 * run)
        starts = [base + (at + s) * (2 * run * spots) for s in range(count)]
        store_rows(table, got, starts, run)


def halo_kernel(split, kv_ref, ids_ref, *refs):
    flat, (weight_ref, left_ref, down_ref, up_ref, picked) = refs[: sum(split)], refs[sum(split) :]
    pieces, at = [], 0
    for count in split:
        pieces.append(flat[at : at + count])
        at += count
    project_pieces(pieces, kv_ref, weight_ref, left_ref, len(split))
    halo = ids_ref.shape[0]

    def move(i, carry):
        base = i * 32
        for j in range(32):
            row = left_ref[pl.ds(pl.multiple_of(ids_ref[base + j], 2), 2), :]
            picked[pl.ds(pl.multiple_of((base + j) * 2, 2), 2), :] = row
        return carry

    lax.fori_loop(0, halo // 32, move, 0)
    for side, ref in enumerate((down_ref, up_ref)):
        for half in range(2):
            rows = picked[pl.ds(side * halo + half, halo // 2, stride=2), :]
            ref[:, half * 128 : half * 128 + 128] = rows.astype(BF)


def halo_call(pieces, kvs, ids, weight):
    split = tuple(len(p) for p in pieces)
    flat = [a for p in pieces for a in p]
    chans = weight.shape[0]
    halo = ids.shape[0]
    rows = sum(a.shape[0] * a.shape[1] for a in flat)
    whole = pl.BlockSpec(memory_space=pltpu.VMEM)
    return pl.pallas_call(
        functools.partial(halo_kernel, split),
        out_shape=(
            jax.ShapeDtypeStruct((2 * rows, 128), F32),
            jax.ShapeDtypeStruct((halo // 2, chans), BF),
            jax.ShapeDtypeStruct((halo // 2, chans), BF),
        ),
        grid_spec=pltpu.PrefetchScalarGridSpec(
            num_scalar_prefetch=2,
            grid=(),
            in_specs=[whole] * (len(flat) + 1),
            out_specs=(whole,) * 3,
            scratch_shapes=[pltpu.VMEM((2 * halo, 128), F32)],
        ),
        compiler_params=params(16),
        cost_estimate=pl.CostEstimate(flops=2 * rows * chans * chans, transcendentals=0, bytes_accessed=8 << 20),
        name="halo",
    )(kvs, ids, *flat, weight)


def right_kernel(split, kv_ref, dst_ref, *refs):
    flat, (weight_ref, out_ref, got_ref, table) = refs[: sum(split)], refs[sum(split) :]
    pieces, at = [], 0
    for count in split:
        pieces.append(flat[at : at + count])
        at += count
    for kv, at, ref in pairs_of(pieces):
        out_ref[at : at + ref.shape[0], kv_ref[kv]] = ref[...]
    project_pieces(pieces, kv_ref, weight_ref, table, len(split))

    def move(i, carry):
        base = i * 32
        for j in range(32):
            row = table[pl.ds(pl.multiple_of(dst_ref[base + j], 2), 2), :]
            got_ref[pl.ds(pl.multiple_of((base + j) * 2, 2), 2), :] = row
        return carry

    lax.fori_loop(0, dst_ref.shape[0] // 32, move, 0)


def right_call(pieces, kvs, dst, weight):
    split = tuple(len(p) for p in pieces)
    flat = [a for p in pieces for a in p]
    count, run, chans = pieces[0][0].shape
    edges = dst.shape[0]
    rows = sum(a.shape[0] * a.shape[1] for a in flat)
    whole = pl.BlockSpec(memory_space=pltpu.VMEM)
    return pl.pallas_call(
        functools.partial(right_kernel, split),
        out_shape=(
            jax.ShapeDtypeStruct((count, len(split), run, chans), BF),
            jax.ShapeDtypeStruct((2 * edges, 128), F32),
        ),
        grid_spec=pltpu.PrefetchScalarGridSpec(
            num_scalar_prefetch=2,
            grid=(),
            in_specs=[whole] * (len(flat) + 1),
            out_specs=(whole,) * 2,
            scratch_shapes=[pltpu.VMEM((2 * rows, 128), F32)],
        ),
        compiler_params=params(20),
        cost_estimate=pl.CostEstimate(flops=2 * rows * chans * chans, transcendentals=0, bytes_accessed=8 << 20),
        name="right",
    )(kvs, dst, *flat, weight)


def edges_kernel(src_ref, count_ref, left_ref, lower_ref, upper_ref, got_ref, map_ref, out_ref, table, pair):
    step = pl.program_id(0)
    own = left_ref.shape[0]
    ghosts = lower_ref.shape[0]
    block = out_ref.shape[1]

    @pl.when(step == 0)
    def _():
        table[:own, :] = left_ref[...]
        for side, ref in enumerate((lower_ref, upper_ref)):
            value = ref[...].astype(F32)
            store_rows(table, value, [own + side * 2 * ghosts], ghosts)

    def some_edges(i, carry):
        base = i * 32
        for j in range(32):
            at = step * block + base + j
            a = table[pl.ds(pl.multiple_of(src_ref[at], 2), 2), :]
            b = got_ref[pl.ds(pl.multiple_of((base + j) * 2, 2), 2), :]
            pair[pl.ds(pl.multiple_of((base + j) * 2, 2), 2), :] = a * b
        return carry

    lax.fori_loop(0, block // 32, some_edges, 0)
    total = None
    for half in range(2):
        value = pair[pl.ds(half, block, stride=2), :].astype(BF)
        part = lax.dot_general(
            map_ref[:, half * 128 : half * 128 + 128],
            value,
            (((1,), (1,)), ((), ())),
            preferred_element_type=F32,
        )
        total = part if total is None else total + part
    at = step * block + lax.broadcasted_iota(jnp.int32, (1, block), 1)
    out_ref[...] = jnp.where(at < count_ref[0], total, 0.0).astype(BF)


def edges_call(src, count, left, lower, upper, got, mapping):
    edges = src.shape[0]
    orb = mapping.shape[0]
    ghosts = lower.shape[0]
    whole = lambda a: pl.BlockSpec(a.shape, lambda i, *_: (0, 0))
    return pl.pallas_call(
        edges_kernel,
        out_shape=jax.ShapeDtypeStruct((orb, edges), BF),
        grid_spec=pltpu.PrefetchScalarGridSpec(
            num_scalar_prefetch=2,
            grid=(edges // TILE,),
            in_specs=[
                whole(left),
                whole(lower),
                whole(upper),
                pl.BlockSpec((2 * TILE, 128), lambda i, *_: (i, 0)),
                whole(mapping),
            ],
            out_specs=pl.BlockSpec((orb, TILE), lambda i, *_: (0, i)),
            scratch_shapes=[
                pltpu.VMEM((left.shape[0] + 4 * ghosts, 128), F32),
                pltpu.VMEM((2 * TILE, 128), F32),
            ],
        ),
        compiler_params=params(24),
        cost_estimate=pl.CostEstimate(flops=2 * edges * 256 * orb, transcendentals=0, bytes_accessed=8 << 20),
        name="edges",
    )(src, count, left, lower, upper, got, mapping)


def exchange(pieces, axes):
    return lax.all_to_all(pieces, axes, 0, 0, tiled=True)


def shift(value, axis, by):
    count = lax.axis_size(axis)
    return lax.ppermute(value, axis, [(i, (i + by) % count) for i in range(count)])


def local(
    particle_traits,
    particle_coordinates,
    kspace_vectors,
    learned_kspace_filter,
    spatial_home,
    following_halo_lines,
    previous_halo_lines,
    sender_projection,
    receiver_projection,
    pair_channel_mapping,
    vertex_rescaling_gain,
    link_sender_line,
    link_receiver_particle,
    active_link_tally,
):
    n_atoms = lax.axis_size(ATOM_AXES)
    n_planes = lax.axis_size(PLANE_AXES)
    n_x = lax.axis_size("x")
    n_kvec = lax.axis_size(KV_AXES)
    core = lax.axis_index("core")
    x, yl = lax.axis_index("x"), lax.axis_index("yl")
    atoms, chans = particle_traits.shape
    kdev = kspace_vectors.shape[1]
    norm_scale = 1.0 / math.sqrt(atoms * n_atoms * kdev * n_kvec)
    share = atoms // n_kvec
    run = atoms // n_atoms // n_kvec
    piece = kdev // n_atoms
    core_word = core.astype(jnp.int32)[None]

    keep, send = struct_call(core_word, particle_coordinates, kspace_vectors, particle_traits, n_planes)
    chip = (keep.astype(F32) + shift(send, "core", 1).astype(F32)).astype(BF)
    spread = exchange(chip, PLANE_AXES)

    home = spatial_home[0]
    goal = home // run % n_kvec
    tile = (1 - (goal // n_x + yl) % 2) * n_x + (goal - x + 2) % n_x
    own_tile = n_x + 2
    places = tile * share + home // (run * n_kvec) * run + home % run
    want = (places - own_tile * share)[None, :]
    ordered, krhs, feats = order_call(
        places, want, core_word, particle_coordinates, kspace_vectors, particle_traits, share
    )

    struct = jnp.sum(spread.astype(F32), axis=0)
    at = (core * n_planes + lax.axis_index(PLANE_AXES)) * piece
    filter_piece = lax.dynamic_slice_in_dim(learned_kspace_filter, at, piece, 0)
    filtered = (filter_piece[None] * struct * norm_scale).astype(BF)
    own = exchange(jnp.broadcast_to(filtered[None], (n_planes,) + filtered.shape), PLANE_AXES)
    other = shift(own, "core", 1)

    parts = []
    for j in (0, 1, 3, 2, 4, 5, 7, own_tile):
        value = update_call(j, ordered, krhs, own, other)
        if j != own_tile:
            dy, dx = 1 - j // n_x, (j % n_x + 2) % n_x
            pairs = [
                (a * n_x + b, (a + dy) % 2 * n_x + (b + dx) % n_x) for a in range(2) for b in range(n_x)
            ]
            value = lax.ppermute(value, KV_AXES, pairs)
        parts.append(value)
    node = node_call(parts, feats, vertex_rescaling_gain[None, :])
    mine = exchange(node.reshape(n_atoms, run, chans), ATOM_AXES)

    half = n_atoms // 2
    across = shift(mine, "yl", 1)
    before = shift(mine, "x", 1)
    after = shift(mine, "x", -1)
    far = (shift(before[:half], "x", 1), shift(after[half:], "x", -1))
    across_before = shift(across, "x", 1)
    across_after = shift(after, "yl", 1)
    across_far = tuple(shift(a, "yl", 1) for a in far)
    pieces = ((mine,), (after,), far, (before,), (across,), (across_after,), across_far, (across_before,))
    offsets = jnp.arange(n_kvec, dtype=jnp.int32)
    kvs = (yl + offsets // n_x) % 2 * n_x + (x + offsets % n_x) % n_x

    ids = jnp.concatenate([following_halo_lines[0], previous_halo_lines[0]]) * 2
    left, for_next, for_previous = halo_call(pieces, kvs, ids, sender_projection)
    lower = shift(for_next, ATOM_AXES, 1)
    upper = shift(for_previous, ATOM_AXES, -1)
    partition_rows, got = right_call(pieces, kvs, link_receiver_particle * 2, receiver_projection)
    orbital_blocks = edges_call(
        link_sender_line * 2, active_link_tally, left, lower, upper, got, pair_channel_mapping
    )
    return (orbital_blocks, partition_rows.reshape(atoms, chans))


def solution(mesh):
    fine = Mesh(mesh.devices.reshape(8, 2, 2, 2, 4), ATOM_AXES + KV_AXES)
    every = ATOM_AXES + KV_AXES
    placed = (
        P(ATOM_AXES, None),
        P(None, ATOM_AXES),
        P(None, KV_AXES),
        P(KV_AXES, None),
        P(ATOM_AXES, None),
        P(ATOM_AXES, None),
        P(ATOM_AXES, None),
        P(),
        P(),
        P(),
        P(),
        P(every),
        P(every),
        P(every),
    )
    return jax.shard_map(
        local,
        mesh=fine,
        in_specs=placed,
        out_specs=(P(None, every), P(ATOM_AXES, None)),
        check_vma=False,
    )
```

time: 218 us -> 173 us (0.79)
  the two profiles are of different devices: /device:TPU:7 before, /device:TPU:1 now
where the time goes in v1:
time: 173 us
  Pallas kernels  51.9 us (30%)
  waiting for transfers between devices  51.7 us (30%)
  starting transfers between devices  41.6 us (24%)
  blocking collectives  20.6 us (12%)
  local copies, waits for them, and re-layouts  4.02 us (2%)
    all_to_all x2, waiting for transfers between devices, exchange(): return lax.all_to_all(pieces, axes, 0, 0, tiled=True)  23.2 us
    all_to_all x1, blocking collectives, exchange(): return lax.all_to_all(pieces, axes, 0, 0, tiled=True)  20.6 us
    ppermute x13, waiting for transfers between devices, shift(): lax.ppermute(value, axis, [(i, (i + by) % count) for i in range(count)])  19.4 us
    ppermute x13, starting transfers between devices, shift(): lax.ppermute(value, axis, [(i, (i + by) % count) for i in range(count)])  19.1 us
    pallas_call x1, Pallas kernels, struct_call(): pl.pallas_call(struct_kernel, out_shape=[jax.ShapeDtypeStruct(shape, BF)]...  13.2 us
    all_to_all x2, starting transfers between devices, exchange(): return lax.all_to_all(pieces, axes, 0, 0, tiled=True)  12.8 us
    pallas_call x8, Pallas kernels, update_call(): pl.pallas_call(update_kernel, out_shape=jax.ShapeDtypeStruct((TILE, chans...  12.7 us
    ppermute x7, starting transfers between devices, local(): value = lax.ppermute(value, KV_AXES, pairs)  9.68 us
  transfers between devices with their start and end apart: 22, of which 13 were waited for; matrix products, arithmetic and copies ran while one was open for 0% of the time, Pallas kernels for 15%

profile of v1, /device:TPU:1, one launch (start us, length us, event | category | flops | bytes accessed | tf_op | source)
XLA Modules:
  0.0 172.8 jit_solution(1504511113622467446)
XLA Ops:
  0.7 1.6 copy-done.5
  3.8 13.2 %struct.1 = (bf16[16,2,16,256]{3,2,1,0:T(8,128)(2,1)S(1)}, bf16[16,2,16,256]{3,2,1,0:T(8,128)(2,1)S(1)}) custom-call(s32[1]{0:T(128)} %bitcast.3.core_ref, f32[3,4096]{1,0:T(4,128)S(1)} %copy-done.7, f32[3,512]{1,0:T(4,128)S(1)} %copy-done.9, bf16[4096,256]{1,0:T(8,128)(2,1)S(1)} %copy-done.5), custom_call_target="tpu_custom_call" | custom-call | flops 3221225472 | bytes 4194304 | tf_op jit(solution)/shard_map/struct/pallas_call | solution.py:119
  17.1 3.3 %collective-permute-start = (bf16[16,2,16,256]{3,2,1,0:T(8,128)(2,1)S(1)}, bf16[16,2,16,256]{3,2,1,0:T(8,128)(2,1)S(1)}, u32[]{:S(2)}, u32[]{:S(2)}) collective-permute-start(bf16[16,2,16,256]{3,2,1,0:T(8,128)(2,1)S(1)} %get-tuple-element.15), channel_id=1, source_target_pairs={{0,8},{8,0},{1,9},{9,1},{2,10},{10,2},{3,11},{11,3},{4,12},{12,4},... | collective-permute-start | bytes 786440 | tf_op jit(solution)/shard_map/ppermute | solution.py:475
  22.3 9.2 %all-to-all-start = ((bf16[16,2,16,256]{3,2,1,0:T(8,128)(2,1)}), bf16[16,2,16,256]{3,2,1,0:T(8,128)(2,1)S(1)}, u32[]{:S(2)}, u32[]{:S(2)}) async-start(bf16[16,2,16,256]{3,2,1,0:T(8,128)(2,1)} %add_convert_fusion), calls=%async_computation | async-start | bytes 524288 | tf_op jit(solution)/shard_map/all_to_all | solution.py:470
  31.6 12.5 %all-to-all-done = bf16[16,2,16,256]{3,2,1,0:T(8,128)(2,1)S(1)} async-done(((bf16[16,2,16,256]{3,2,1,0:T(8,128)(2,1)}), bf16[16,2,16,256]{3,2,1,0:T(8,128)(2,1)S(1)}, u32[]{:S(2)}, u32[]{:S(2)}) %all-to-all-start) | async-done | bytes 262176 | tf_op jit(solution)/shard_map/all_to_all | solution.py:470
  44.8 3.5 %all-to-all-start.1 = ((bf16[16,2,16,256]{3,2,1,0:T(8,128)(2,1)}), bf16[16,2,16,256]{3,2,1,0:T(8,128)(2,1)S(1)}, u32[]{:S(2)}, u32[]{:S(2)}) async-start(bf16[16,2,16,256]{3,2,1,0:T(8,128)(2,1)} %broadcast_in_dim.7), calls=%async_computation.1 | async-start | bytes 524288 | tf_op jit(solution)/shard_map/all_to_all | solution.py:470
  48.8 10.8 %all-to-all-done.1.own_ref = bf16[16,2,16,256]{3,2,1,0:T(8,128)(2,1)S(1)} async-done(((bf16[16,2,16,256]{3,2,1,0:T(8,128)(2,1)}), bf16[16,2,16,256]{3,2,1,0:T(8,128)(2,1)S(1)}, u32[]{:S(2)}, u32[]{:S(2)}) %all-to-all-start.1) | async-done | bytes 262176 | tf_op jit(solution)/shard_map/all_to_all | solution.py:470
  59.6 3.7 %collective-permute-start.1 = (bf16[16,2,16,256]{3,2,1,0:T(8,128)(2,1)S(1)}, bf16[16,2,16,256]{3,2,1,0:T(8,128)(2,1)S(1)}, u32[]{:S(2)}, u32[]{:S(2)}) collective-permute-start(bf16[16,2,16,256]{3,2,1,0:T(8,128)(2,1)S(1)} %all-to-all-done.1.own_ref), channel_id=1, source_target_pairs={{0,8},{8,0},{1,9},{9,1},{2,10},{10,2},{3,11},{11,3},{4,12},{12,4},... | collective-permute-start | bytes 786440 | tf_op jit(solution)/shard_map/ppermute | solution.py:475
  63.3 7.6 %order.1 = (bf16[4096,128]{1,0:T(8,128)(2,1)S(1)}, bf16[128,512]{1,0:T(8,128)(2,1)S(1)}, bf16[512,256]{1,0:T(8,128)(2,1)S(1)}) custom-call(s32[4096]{0:T(1024)S(1)} %fusion.11.place_ref, s32[1]{0:T(128)} %bitcast.3.core_ref, f32[3,4096]{1,0:T(4,128)S(1)} %copy-done.8, f32[3,512]{1,0:T(4,128)S(1)} %copy-done.10, s32[1,4096]{1,0:T(1,128)S(1)} %fusion.20.want_ref, ...), custom_call_target="tpu_custom_call" | custom-call | flops 2147483648 | bytes 12582912 | tf_op jit(solution)/shard_map/order/pallas_call | solution.py:185
  88.2 2.6 %collective-permute-start.3 = (bf16[512,256]{1,0:T(8,128)(2,1)S(1)}, bf16[512,256]{1,0:T(8,128)(2,1)S(1)}, u32[]{:S(2)}, u32[]{:S(2)}) collective-permute-start(bf16[512,256]{1,0:T(8,128)(2,1)S(1)} %update.9), channel_id=1, source_target_pairs={{0,7},{1,4},{2,5},{3,6},{4,3},{5,0},{6,1},{7,2},{8,15},{9,12},{10,... | collective-permute-start | bytes 786440 | tf_op jit(solution)/shard_map/ppermute | solution.py:537
  94.8 7.4 %collective-permute-done.3.refs_1_ = bf16[512,256]{1,0:T(8,128)(2,1)S(1)} collective-permute-done((bf16[512,256]{1,0:T(8,128)(2,1)S(1)}, bf16[512,256]{1,0:T(8,128)(2,1)S(1)}, u32[]{:S(2)}, u32[]{:S(2)}) %collective-permute-start.3) | collective-permute-done | bytes 262176 | tf_op jit(solution)/shard_map/ppermute | solution.py:537
  103.3 20.6 %all_to_all.15.refs_0_ = bf16[32,16,256]{2,1,0:T(8,128)(2,1)S(1)} all-to-all(bf16[32,16,256]{2,1,0:T(8,128)(2,1)S(1)} %bitcast.7), channel_id=1, replica_groups=mesh['z'=8,'yh'=2,'core'=2,'yl'=2,'x'=4] {'z','yh','core'}, dimensions={0} | all-to-all | bytes 524288 | tf_op jit(solution)/shard_map/all_to_all | solution.py:470
  123.9 1.8 %collective-permute-start.10 = (bf16[32,16,256]{2,1,0:T(8,128)(2,1)S(1)}, bf16[32,16,256]{2,1,0:T(8,128)(2,1)S(1)}, u32[]{:S(2)}, u32[]{:S(2)}) collective-permute-start(bf16[32,16,256]{2,1,0:T(8,128)(2,1)S(1)} %all_to_all.15.refs_0_), channel_id=1, source_target_pairs={{0,1},{1,2},{2,3},{3,0},{4,5},{5,6},{6,7},{7,4},{8,9},{9,10},{10,1... | collective-permute-start | bytes 786440 | tf_op jit(solution)/shard_map/ppermute | solution.py:475
  125.7 2.4 %collective-permute-start.9 = (bf16[32,16,256]{2,1,0:T(8,128)(2,1)S(1)}, bf16[32,16,256]{2,1,0:T(8,128)(2,1)S(1)}, u32[]{:S(2)}, u32[]{:S(2)}) collective-permute-start(bf16[32,16,256]{2,1,0:T(8,128)(2,1)S(1)} %all_to_all.15.refs_0_), channel_id=1, source_target_pairs={{0,3},{1,0},{2,1},{3,2},{4,7},{5,4},{6,5},{7,6},{8,11},{9,8},{10,9... | collective-permute-start | bytes 786440 | tf_op jit(solution)/shard_map/ppermute | solution.py:475
  128.6 5.8 %collective-permute-done.10.refs_4_ = bf16[32,16,256]{2,1,0:T(8,128)(2,1)S(1)} collective-permute-done((bf16[32,16,256]{2,1,0:T(8,128)(2,1)S(1)}, bf16[32,16,256]{2,1,0:T(8,128)(2,1)S(1)}, u32[]{:S(2)}, u32[]{:S(2)}) %collective-permute-start.10) | collective-permute-done | bytes 262176 | tf_op jit(solution)/shard_map/ppermute | solution.py:475
  134.5 2.7 %collective-permute-start.12 = (bf16[16,16,256]{2,1,0:T(8,128)(2,1)S(1)}, bf16[16,16,256]{2,1,0:T(8,128)(2,1)S(1)}, u32[]{:S(2)}, u32[]{:S(2)}) collective-permute-start(bf16[16,16,256]{2,1,0:T(8,128)(2,1)S(1)} %slice.9), channel_id=1, source_target_pairs={{0,3},{1,0},{2,1},{3,2},{4,7},{5,4},{6,5},{7,6},{8,11},{9,8},{10,9... | collective-permute-start | bytes 393224 | tf_op jit(solution)/shard_map/ppermute | solution.py:475
  137.7 1.8 %collective-permute-done.11.refs_2_ = bf16[16,16,256]{2,1,0:T(8,128)(2,1)S(1)} collective-permute-done((bf16[16,16,256]{2,1,0:T(8,128)(2,1)S(1)}, bf16[16,16,256]{2,1,0:T(8,128)(2,1)S(1)}, u32[]{:S(2)}, u32[]{:S(2)}) %collective-permute-start.11) | collective-permute-done | bytes 131104 | tf_op jit(solution)/shard_map/ppermute | solution.py:475
  141.7 1.9 %collective-permute-done.14.refs_6_ = bf16[32,16,256]{2,1,0:T(8,128)(2,1)S(1)} collective-permute-done((bf16[32,16,256]{2,1,0:T(8,128)(2,1)S(1)}, bf16[32,16,256]{2,1,0:T(8,128)(2,1)S(1)}, u32[]{:S(2)}, u32[]{:S(2)}) %collective-permute-start.14) | collective-permute-done | bytes 262176 | tf_op jit(solution)/shard_map/ppermute | solution.py:475
  146.4 2.8 %collective-permute-done.16.refs_8_ = bf16[16,16,256]{2,1,0:T(8,128)(2,1)S(1)} collective-permute-done((bf16[16,16,256]{2,1,0:T(8,128)(2,1)S(1)}, bf16[16,16,256]{2,1,0:T(8,128)(2,1)S(1)}, u32[]{:S(2)}, u32[]{:S(2)}) %collective-permute-start.16) | collective-permute-done | bytes 131104 | tf_op jit(solution)/shard_map/ppermute | solution.py:475
  149.2 2.5 %halo.1 = (f32[8192,128]{1,0:T(8,128)S(1)}, bf16[512,256]{1,0:T(8,128)(2,1)S(1)}, bf16[512,256]{1,0:T(8,128)(2,1)S(1)}) custom-call(s32[8]{0:T(128)S(1)} %fusion.27.kv_ref, s32[1024]{0:T(1024)S(1)} %add_multiply_fusion.ids_ref, bf16[32,16,256]{2,1,0:T(8,128)(2,1)S(1)} %all_to_all.15.refs_0_, bf16[32,16,256]{2,1,0:T(8,128)(2,1)S(1)} %collective-permute-done.9.refs_1_, ...), custom_call_target="tpu_custom_call" | custom-call | flops 536870912 | bytes 8388608 | tf_op jit(solution)/shard_map/halo/pallas_call | solution.py:336
  151.7 2.8 %collective-permute-start.18 = (bf16[512,256]{1,0:T(8,128)(2,1)S(1)}, bf16[512,256]{1,0:T(8,128)(2,1)S(1)}, u32[]{:S(2)}, u32[]{:S(2)}) collective-permute-start(bf16[512,256]{1,0:T(8,128)(2,1)S(1)} %get-tuple-element.18), channel_id=1, source_target_pairs={{0,8},{8,16},{16,24},{24,32},{32,40},{40,48},{48,56},{56,64},{64,7... | collective-permute-start | bytes 786440 | tf_op jit(solution)/shard_map/ppermute | solution.py:475
  154.5 7.0 %right.1 = (bf16[32,8,16,256]{3,2,1,0:T(8,128)(2,1)}, f32[8192,128]{1,0:T(8,128)S(1)}) custom-call(s32[8]{0:T(128)S(1)} %fusion.27.kv_ref, s32[4096]{0:T(1024)S(1)} %broadcast_multiply_fusion.dst_ref, bf16[32,16,256]{2,1,0:T(8,128)(2,1)S(1)} %all_to_all.15.refs_0_, bf16[32,16,256]{2,1,0:T(8,128)(2,1)S(1)} %collective-permute-done.9.refs_1_, ...), custom_call_target="tpu_custom_call" | custom-call | flops 536870912 | bytes 8388608 | tf_op jit(solution)/shard_map/right/pallas_call | solution.py:383
  161.6 3.0 %collective-permute-done.19.upper_ref = bf16[512,256]{1,0:T(8,128)(2,1)S(1)} collective-permute-done((bf16[512,256]{1,0:T(8,128)(2,1)S(1)}, bf16[512,256]{1,0:T(8,128)(2,1)S(1)}, u32[]{:S(2)}, u32[]{:S(2)}) %collective-permute-start.19) | collective-permute-done | bytes 262176 | tf_op jit(solution)/shard_map/ppermute | solution.py:475
  164.6 8.2 %edges.1 = bf16[196,4096]{1,0:T(8,128)(2,1)} custom-call(s32[4096]{0:T(1024)S(1)} %broadcast_multiply_fusion.1.src_ref, s32[1]{0:T(128)S(6)} %copy.16.count_ref, f32[8192,128]{1,0:T(8,128)S(1)} %get-tuple-element.17.left_ref, bf16[512,256]{1,0:T(8,128)(2,1)S(1)} %collective-permute-done.18.lower_ref, bf16[512,256]{1,0:T(8,128)(2,1)S(1)} %collective-permute-done.19.upper_ref, ...), custom_call_target="tpu_custom_call" | custom-call | flops 411041792 | bytes 8388608 | tf_op jit(solution)/shard_map/edges/pallas_call | solution.py:444
  (80 shorter events, 32.4 us)
Async XLA Ops:
  17.1 4.4 %collective-permute-start = (bf16[16,2,16,256]{3,2,1,0:T(8,128)(2,1)S(1)}, bf16[16,2,16,256]{3,2,1,0:T(8,128)(2,1)S(1)}, u32[]{:S(2)}, u32[]{:S(2)}) collective-permute-start(bf16[16,2,16,256]{3,2,1,0:T(8,128)(2,1)S(1)} %get-tuple-element.15), channel_id=1, source_target_pairs={{0,8},{8,0},{1,9},{9,1},{2,10},{10,2},{3,11},{11,3},{4,12},{12,4},... | collective-permute-start | bytes 786440 | tf_op jit(solution)/shard_map/ppermute | solution.py:475
  22.3 21.7 %all-to-all-start = ((bf16[16,2,16,256]{3,2,1,0:T(8,128)(2,1)}), bf16[16,2,16,256]{3,2,1,0:T(8,128)(2,1)S(1)}, u32[]{:S(2)}, u32[]{:S(2)}) async-start(bf16[16,2,16,256]{3,2,1,0:T(8,128)(2,1)} %add_convert_fusion), calls=%async_computation | async-start | bytes 524288 | tf_op jit(solution)/shard_map/all_to_all | solution.py:470
  44.8 14.7 %all-to-all-start.1 = ((bf16[16,2,16,256]{3,2,1,0:T(8,128)(2,1)}), bf16[16,2,16,256]{3,2,1,0:T(8,128)(2,1)S(1)}, u32[]{:S(2)}, u32[]{:S(2)}) async-start(bf16[16,2,16,256]{3,2,1,0:T(8,128)(2,1)} %broadcast_in_dim.7), calls=%async_computation.1 | async-start | bytes 524288 | tf_op jit(solution)/shard_map/all_to_all | solution.py:470
  59.6 11.3 %collective-permute-start.1 = (bf16[16,2,16,256]{3,2,1,0:T(8,128)(2,1)S(1)}, bf16[16,2,16,256]{3,2,1,0:T(8,128)(2,1)S(1)}, u32[]{:S(2)}, u32[]{:S(2)}) collective-permute-start(bf16[16,2,16,256]{3,2,1,0:T(8,128)(2,1)S(1)} %all-to-all-done.1.own_ref), channel_id=1, source_target_pairs={{0,8},{8,0},{1,9},{9,1},{2,10},{10,2},{3,11},{11,3},{4,12},{12,4},... | collective-permute-start | bytes 786440 | tf_op jit(solution)/shard_map/ppermute | solution.py:475
  72.5 15.7 %collective-permute-start.8 = (bf16[512,256]{1,0:T(8,128)(2,1)S(1)}, bf16[512,256]{1,0:T(8,128)(2,1)S(1)}, u32[]{:S(2)}, u32[]{:S(2)}) collective-permute-start(bf16[512,256]{1,0:T(8,128)(2,1)S(1)} %update.14), channel_id=1, source_target_pairs={{0,1},{1,2},{2,3},{3,0},{4,5},{5,6},{6,7},{7,4},{8,9},{9,10},{10,1... | collective-permute-start | bytes 786440 | tf_op jit(solution)/shard_map/ppermute | solution.py:537
  75.4 15.4 %collective-permute-start.7 = (bf16[512,256]{1,0:T(8,128)(2,1)S(1)}, bf16[512,256]{1,0:T(8,128)(2,1)S(1)}, u32[]{:S(2)}, u32[]{:S(2)}) collective-permute-start(bf16[512,256]{1,0:T(8,128)(2,1)S(1)} %update.13), channel_id=1, source_target_pairs={{0,3},{1,0},{2,1},{3,2},{4,7},{5,4},{6,5},{7,6},{8,11},{9,8},{10,9... | collective-permute-start | bytes 786440 | tf_op jit(solution)/shard_map/ppermute | solution.py:537
  78.5 14.9 %collective-permute-start.6 = (bf16[512,256]{1,0:T(8,128)(2,1)S(1)}, bf16[512,256]{1,0:T(8,128)(2,1)S(1)}, u32[]{:S(2)}, u32[]{:S(2)}) collective-permute-start(bf16[512,256]{1,0:T(8,128)(2,1)S(1)} %update.12), channel_id=1, source_target_pairs={{0,2},{1,3},{2,0},{3,1},{4,6},{5,7},{6,4},{7,5},{8,10},{9,11},{10,... | collective-permute-start | bytes 786440 | tf_op jit(solution)/shard_map/ppermute | solution.py:537
  81.8 11.7 %collective-permute-start.5 = (bf16[512,256]{1,0:T(8,128)(2,1)S(1)}, bf16[512,256]{1,0:T(8,128)(2,1)S(1)}, u32[]{:S(2)}, u32[]{:S(2)}) collective-permute-start(bf16[512,256]{1,0:T(8,128)(2,1)S(1)} %update.11), channel_id=1, source_target_pairs={{0,4},{1,5},{2,6},{3,7},{4,0},{5,1},{6,2},{7,3},{8,12},{9,13},{10,... | collective-permute-start | bytes 786440 | tf_op jit(solution)/shard_map/ppermute | solution.py:537
  83.9 10.9 %collective-permute-start.4 = (bf16[512,256]{1,0:T(8,128)(2,1)S(1)}, bf16[512,256]{1,0:T(8,128)(2,1)S(1)}, u32[]{:S(2)}, u32[]{:S(2)}) collective-permute-start(bf16[512,256]{1,0:T(8,128)(2,1)S(1)} %update.10), channel_id=1, source_target_pairs={{0,5},{1,6},{2,7},{3,4},{4,1},{5,2},{6,3},{7,0},{8,13},{9,14},{10,... | collective-permute-start | bytes 786440 | tf_op jit(solution)/shard_map/ppermute | solution.py:537
  88.2 13.9 %collective-permute-start.3 = (bf16[512,256]{1,0:T(8,128)(2,1)S(1)}, bf16[512,256]{1,0:T(8,128)(2,1)S(1)}, u32[]{:S(2)}, u32[]{:S(2)}) collective-permute-start(bf16[512,256]{1,0:T(8,128)(2,1)S(1)} %update.9), channel_id=1, source_target_pairs={{0,7},{1,4},{2,5},{3,6},{4,3},{5,0},{6,1},{7,2},{8,15},{9,12},{10,... | collective-permute-start | bytes 786440 | tf_op jit(solution)/shard_map/ppermute | solution.py:537
  90.8 11.8 %collective-permute-start.2 = (bf16[512,256]{1,0:T(8,128)(2,1)S(1)}, bf16[512,256]{1,0:T(8,128)(2,1)S(1)}, u32[]{:S(2)}, u32[]{:S(2)}) collective-permute-start(bf16[512,256]{1,0:T(8,128)(2,1)S(1)} %update.8), channel_id=1, source_target_pairs={{0,6},{1,7},{2,4},{3,5},{4,2},{5,3},{6,0},{7,1},{8,14},{9,15},{10,... | collective-permute-start | bytes 786440 | tf_op jit(solution)/shard_map/ppermute | solution.py:537
  93.4 55.8 %copy-start.1 = (bf16[256,256]{1,0:T(8,128)(2,1)S(1)}, bf16[256,256]{1,0:T(8,128)(2,1)}, u32[]{:S(2)}) copy-start(bf16[256,256]{1,0:T(8,128)(2,1)} %refs_10_.2) | copy-start | bytes 393220
  103.2 51.3 %copy-start.13 = (s32[4096]{0:T(1024)S(1)}, s32[4096]{0:T(1024)}, u32[]{:S(2)}) copy-start(s32[4096]{0:T(1024)} %param.25) | copy-start | bytes 49156
  123.9 10.5 %collective-permute-start.10 = (bf16[32,16,256]{2,1,0:T(8,128)(2,1)S(1)}, bf16[32,16,256]{2,1,0:T(8,128)(2,1)S(1)}, u32[]{:S(2)}, u32[]{:S(2)}) collective-permute-start(bf16[32,16,256]{2,1,0:T(8,128)(2,1)S(1)} %all_to_all.15.refs_0_), channel_id=1, source_target_pairs={{0,1},{1,2},{2,3},{3,0},{4,5},{5,6},{6,7},{7,4},{8,9},{9,10},{10,1... | collective-permute-start | bytes 786440 | tf_op jit(solution)/shard_map/ppermute | solution.py:475
  125.7 8.8 %collective-permute-start.9 = (bf16[32,16,256]{2,1,0:T(8,128)(2,1)S(1)}, bf16[32,16,256]{2,1,0:T(8,128)(2,1)S(1)}, u32[]{:S(2)}, u32[]{:S(2)}) collective-permute-start(bf16[32,16,256]{2,1,0:T(8,128)(2,1)S(1)} %all_to_all.15.refs_0_), channel_id=1, source_target_pairs={{0,3},{1,0},{2,1},{3,2},{4,7},{5,4},{6,5},{7,6},{8,11},{9,8},{10,9... | collective-permute-start | bytes 786440 | tf_op jit(solution)/shard_map/ppermute | solution.py:475
  128.1 9.6 %collective-permute-start.13 = (bf16[32,16,256]{2,1,0:T(8,128)(2,1)S(1)}, bf16[32,16,256]{2,1,0:T(8,128)(2,1)S(1)}, u32[]{:S(2)}, u32[]{:S(2)}) collective-permute-start(bf16[32,16,256]{2,1,0:T(8,128)(2,1)S(1)} %all_to_all.15.refs_0_), channel_id=1, source_target_pairs={{0,4},{4,0},{1,5},{5,1},{2,6},{6,2},{3,7},{7,3},{8,12},{12,8},{9,1... | collective-permute-start | bytes 786440 | tf_op jit(solution)/shard_map/ppermute | solution.py:475
  134.4 5.1 %collective-permute-start.11 = (bf16[16,16,256]{2,1,0:T(8,128)(2,1)S(1)}, bf16[16,16,256]{2,1,0:T(8,128)(2,1)S(1)}, u32[]{:S(2)}, u32[]{:S(2)}) collective-permute-start(bf16[16,16,256]{2,1,0:T(8,128)(2,1)S(1)} %slice.8), channel_id=1, source_target_pairs={{0,1},{1,2},{2,3},{3,0},{4,5},{5,6},{6,7},{7,4},{8,9},{9,10},{10,1... | collective-permute-start | bytes 393224 | tf_op jit(solution)/shard_map/ppermute | solution.py:475
  134.5 5.4 %collective-permute-start.12 = (bf16[16,16,256]{2,1,0:T(8,128)(2,1)S(1)}, bf16[16,16,256]{2,1,0:T(8,128)(2,1)S(1)}, u32[]{:S(2)}, u32[]{:S(2)}) collective-permute-start(bf16[16,16,256]{2,1,0:T(8,128)(2,1)S(1)} %slice.9), channel_id=1, source_target_pairs={{0,3},{1,0},{2,1},{3,2},{4,7},{5,4},{6,5},{7,6},{8,11},{9,8},{10,9... | collective-permute-start | bytes 393224 | tf_op jit(solution)/shard_map/ppermute | solution.py:475
  137.3 6.3 %collective-permute-start.14 = (bf16[32,16,256]{2,1,0:T(8,128)(2,1)S(1)}, bf16[32,16,256]{2,1,0:T(8,128)(2,1)S(1)}, u32[]{:S(2)}, u32[]{:S(2)}) collective-permute-start(bf16[32,16,256]{2,1,0:T(8,128)(2,1)S(1)} %collective-permute-done.9.refs_1_), channel_id=1, source_target_pairs={{0,4},{4,0},{1,5},{5,1},{2,6},{6,2},{3,7},{7,3},{8,12},{12,8},{9,1... | collective-permute-start | bytes 786440 | tf_op jit(solution)/shard_map/ppermute | solution.py:475
  137.7 7.3 %collective-permute-start.17 = (bf16[32,16,256]{2,1,0:T(8,128)(2,1)S(1)}, bf16[32,16,256]{2,1,0:T(8,128)(2,1)S(1)}, u32[]{:S(2)}, u32[]{:S(2)}) collective-permute-start(bf16[32,16,256]{2,1,0:T(8,128)(2,1)S(1)} %collective-permute-done.13.refs_5_), channel_id=1, source_target_pairs={{0,1},{1,2},{2,3},{3,0},{4,5},{5,6},{6,7},{7,4},{8,9},{9,10},{10,1... | collective-permute-start | bytes 786440 | tf_op jit(solution)/shard_map/ppermute | solution.py:475
  139.5 6.9 %collective-permute-start.15 = (bf16[16,16,256]{2,1,0:T(8,128)(2,1)S(1)}, bf16[16,16,256]{2,1,0:T(8,128)(2,1)S(1)}, u32[]{:S(2)}, u32[]{:S(2)}) collective-permute-start(bf16[16,16,256]{2,1,0:T(8,128)(2,1)S(1)} %collective-permute-done.11.refs_2_), channel_id=1, source_target_pairs={{0,4},{4,0},{1,5},{5,1},{2,6},{6,2},{3,7},{7,3},{8,12},{12,8},{9,1... | collective-permute-start | bytes 393224 | tf_op jit(solution)/shard_map/ppermute | solution.py:475
  140.0 9.2 %collective-permute-start.16 = (bf16[16,16,256]{2,1,0:T(8,128)(2,1)S(1)}, bf16[16,16,256]{2,1,0:T(8,128)(2,1)S(1)}, u32[]{:S(2)}, u32[]{:S(2)}) collective-permute-start(bf16[16,16,256]{2,1,0:T(8,128)(2,1)S(1)} %collective-permute-done.12.refs_3_), channel_id=1, source_target_pairs={{0,4},{4,0},{1,5},{5,1},{2,6},{6,2},{3,7},{7,3},{8,12},{12,8},{9,1... | collective-permute-start | bytes 393224 | tf_op jit(solution)/shard_map/ppermute | solution.py:475
  151.7 9.8 %collective-permute-start.18 = (bf16[512,256]{1,0:T(8,128)(2,1)S(1)}, bf16[512,256]{1,0:T(8,128)(2,1)S(1)}, u32[]{:S(2)}, u32[]{:S(2)}) collective-permute-start(bf16[512,256]{1,0:T(8,128)(2,1)S(1)} %get-tuple-element.18), channel_id=1, source_target_pairs={{0,8},{8,16},{16,24},{24,32},{32,40},{40,48},{48,56},{56,64},{64,7... | collective-permute-start | bytes 786440 | tf_op jit(solution)/shard_map/ppermute | solution.py:475
  154.5 10.1 %collective-permute-start.19 = (bf16[512,256]{1,0:T(8,128)(2,1)S(1)}, bf16[512,256]{1,0:T(8,128)(2,1)S(1)}, u32[]{:S(2)}, u32[]{:S(2)}) collective-permute-start(bf16[512,256]{1,0:T(8,128)(2,1)S(1)} %get-tuple-element.19), channel_id=1, source_target_pairs={{0,248},{8,0},{16,8},{24,16},{32,24},{40,32},{48,40},{56,48},{64,5... | collective-permute-start | bytes 786440 | tf_op jit(solution)/shard_map/ppermute | solution.py:475
  (14 other events, 435.2 us)

commit v2 on v1

--- a/solution.py
+++ b/solution.py
@@ -144,9 +144,8 @@
     )(core, coordinates, vectors, feats)
 
 
-def order_kernel(place_ref, core_ref, coord_ref, kvec_ref, want_ref, feat_ref, ordered_ref, krhs_ref, picked_ref, apart, kpart, rows, ordered, acc):
+def order_kernel(place_ref, core_ref, coord_ref, kvec_ref, ordered_ref, krhs_ref, apart, kpart, rows, ordered):
     atoms = coord_ref.shape[1]
-    wanted = picked_ref.shape[0]
     apart[...] = jnp.zeros_like(apart)
     kpart[...] = jnp.zeros_like(kpart)
     store_kspace_parts(kpart, own_first(kvec_ref[...], core_ref[0]))
@@ -163,23 +162,17 @@
         return carry
 
     lax.fori_loop(0, atoms // 32, move, 0)
-    acc[...] = jnp.zeros_like(acc)
-
-    def pick(i, carry):
+
+    def narrow(i, carry):
         span = pl.ds(pl.multiple_of(i * TILE, TILE), TILE)
         ordered_ref[span, :] = ordered[span, :].astype(BF)
-        hot = lax.broadcasted_iota(jnp.int32, (wanted, TILE), 0) == want_ref[:, span]
-        acc[...] += jnp.dot(
-            jnp.where(hot, 1.0, 0.0).astype(BF), feat_ref[span, :], preferred_element_type=F32
-        )
         return carry
 
-    lax.fori_loop(0, atoms // TILE, pick, 0)
-    picked_ref[...] = acc[...].astype(BF)
-
-
-def order_call(places, want, core, coordinates, vectors, feats, wanted):
-    atoms, chans = feats.shape
+    lax.fori_loop(0, atoms // TILE, narrow, 0)
+
+
+def order_call(places, core, coordinates, vectors):
+    atoms = coordinates.shape[1]
     kdev = vectors.shape[1]
     whole = pl.BlockSpec(memory_space=pltpu.VMEM)
     return pl.pallas_call(
@@ -187,25 +180,60 @@
         out_shape=(
             jax.ShapeDtypeStruct((atoms, 128), BF),
             jax.ShapeDtypeStruct((128, kdev), BF),
-            jax.ShapeDtypeStruct((wanted, chans), BF),
         ),
         grid_spec=pltpu.PrefetchScalarGridSpec(
             num_scalar_prefetch=2,
             grid=(),
-            in_specs=[whole] * 4,
-            out_specs=(whole,) * 3,
+            in_specs=[whole] * 2,
+            out_specs=(whole,) * 2,
             scratch_shapes=[
                 pltpu.VMEM((128, TILE), F32),
                 pltpu.VMEM((128, kdev), F32),
                 pltpu.VMEM((atoms, 128), F32),
                 pltpu.VMEM((atoms, 128), F32),
-                pltpu.VMEM((wanted, chans), F32),
             ],
         ),
         compiler_params=params(16),
-        cost_estimate=pl.CostEstimate(flops=4 * atoms * kdev * chans, transcendentals=0, bytes_accessed=12 << 20),
+        cost_estimate=pl.CostEstimate(flops=atoms * kdev * 1024, transcendentals=0, bytes_accessed=4 << 20),
         name="order",
-    )(places, core, coordinates, vectors, want, feats)
+    )(places, core, coordinates, vectors)
+
+
+def pick_kernel(want_ref, feat_ref, picked_ref, acc):
+    wanted = picked_ref.shape[0]
+    hot = lax.broadcasted_iota(jnp.int32, (wanted, TILE), 0) == want_ref[...]
+    got = jnp.dot(jnp.where(hot, 1.0, 0.0).astype(BF), feat_ref[...], preferred_element_type=F32)
+    step = pl.program_id(0)
+
+    @pl.when(step == 0)
+    def _():
+        acc[...] = got
+
+    @pl.when(step > 0)
+    def _():
+        acc[...] += got
+
+    @pl.when(step == pl.num_programs(0) - 1)
+    def _():
+        picked_ref[...] = acc[...].astype(BF)
+
+
+def pick_call(want, feats, wanted):
+    atoms, chans = feats.shape
+    return pl.pallas_call(
+        pick_kernel,
+        out_shape=jax.ShapeDtypeStruct((wanted, chans), BF),
+        grid=(atoms // TILE,),
+        in_specs=[
+            pl.BlockSpec((1, TILE), lambda i: (0, i)),
+            pl.BlockSpec((TILE, chans), lambda i: (i, 0)),
+        ],
+        out_specs=pl.BlockSpec((wanted, chans), lambda i: (0, 0)),
+        scratch_shapes=[pltpu.VMEM((wanted, chans), F32)],
+        compiler_params=params(8),
+        cost_estimate=pl.CostEstimate(flops=2 * atoms * wanted * chans, transcendentals=0, bytes_accessed=3 << 20),
+        name="pick",
+    )(want, feats)
 
 
 def update_kernel(rows_ref, krhs_ref, own_ref, other_ref, out_ref, phase, cosv, sinv):
@@ -249,6 +277,37 @@
         cost_estimate=pl.CostEstimate(flops=4 * TILE * kdev * chans, transcendentals=0, bytes_accessed=1 << 20),
         name="update",
     )(ordered, krhs, own, other)
+
+
+def merge_kernel(starts, cuts, *refs):
+    base_ref, add_refs, out_refs = refs[0], refs[1 : 1 + len(starts)], refs[1 + len(starts) :]
+    at = 0
+    for cut, out_ref in zip(cuts, out_refs):
+        edges = {at, at + cut}
+        for start, ref in zip(starts, add_refs):
+            edges |= {e for e in (start, start + ref.shape[0]) if at < e < at + cut}
+        edges = sorted(edges)
+        for low, high in zip(edges[:-1], edges[1:]):
+            value = base_ref[low:high, :].astype(F32)
+            for start, ref in zip(starts, add_refs):
+                if start <= low and high <= start + ref.shape[0]:
+                    value = value + ref[low - start : high - start, :].astype(F32)
+            out_ref[low - at : high - at, :] = value.astype(BF)
+        at += cut
+
+
+def merge_call(base, addends, cuts):
+    arrays = [base] + [a for a, _ in addends]
+    whole = pl.BlockSpec(memory_space=pltpu.VMEM)
+    return pl.pallas_call(
+        functools.partial(merge_kernel, tuple(s for _, s in addends), cuts),
+        out_shape=[jax.ShapeDtypeStruct((cut, base.shape[1]), BF) for cut in cuts],
+        in_specs=[whole] * len(arrays),
+        out_specs=[whole] * len(cuts),
+        compiler_params=params(4),
+        cost_estimate=pl.CostEstimate(flops=base.size, transcendentals=0, bytes_accessed=1 << 20),
+        name="merge",
+    )(*arrays)
 
 
 def node_kernel(*refs):
@@ -505,7 +564,14 @@
     piece = kdev // n_atoms
     core_word = core.astype(jnp.int32)[None]
 
-    keep, send = struct_call(core_word, particle_coordinates, kspace_vectors, particle_traits, n_planes)
+    in_hbm = lambda a: pltpu.with_memory_space_constraint(a, pltpu.HBM)
+    keep, send = struct_call(
+        core_word,
+        in_hbm(particle_coordinates),
+        in_hbm(kspace_vectors),
+        in_hbm(particle_traits),
+        n_planes,
+    )
     chip = (keep.astype(F32) + shift(send, "core", 1).astype(F32)).astype(BF)
     spread = exchange(chip, PLANE_AXES)
 
@@ -515,9 +581,8 @@
     own_tile = n_x + 2
     places = tile * share + home // (run * n_kvec) * run + home % run
     want = (places - own_tile * share)[None, :]
-    ordered, krhs, feats = order_call(
-        places, want, core_word, particle_coordinates, kspace_vectors, particle_traits, share
-    )
+    ordered, krhs = order_call(places, core_word, particle_coordinates, kspace_vectors)
+    feats = pick_call(want, in_hbm(particle_traits), share)
 
     struct = jnp.sum(spread.astype(F32), axis=0)
     at = (core * n_planes + lax.axis_index(PLANE_AXES)) * piece
@@ -526,16 +591,27 @@
     own = exchange(jnp.broadcast_to(filtered[None], (n_planes,) + filtered.shape), PLANE_AXES)
     other = shift(own, "core", 1)
 
-    parts = []
-    for j in (0, 1, 3, 2, 4, 5, 7, own_tile):
-        value = update_call(j, ordered, krhs, own, other)
-        if j != own_tile:
-            dy, dx = 1 - j // n_x, (j % n_x + 2) % n_x
-            pairs = [
-                (a * n_x + b, (a + dy) % 2 * n_x + (b + dx) % n_x) for a in range(2) for b in range(n_x)
-            ]
-            value = lax.ppermute(value, KV_AXES, pairs)
-        parts.append(value)
+    def towards(dy, dx):
+        return update_call((1 - dy) * n_x + (dx + 2) % n_x, ordered, krhs, own, other)
+
+    middle = share // 2
+    far_across = shift(towards(1, 2), "yl", 1)
+    before_across = shift(towards(1, -1), "yl", 1)
+    after_across = shift(towards(1, 1), "x", 1)
+    far_first, far_second = merge_call(
+        towards(0, 2), ((far_across, 0),), (middle, share - middle)
+    )
+    far_first = shift(far_first, "x", 1)
+    far_second = shift(far_second, "x", -1)
+    (whole_across,) = merge_call(towards(1, 0), ((after_across, 0),), (share,))
+    whole_across = shift(whole_across, "yl", 1)
+    (whole_after,) = merge_call(towards(0, 1), ((far_first, 0),), (share,))
+    whole_after = shift(whole_after, "x", 1)
+    (whole_before,) = merge_call(
+        towards(0, -1), ((before_across, 0), (far_second, middle)), (share,)
+    )
+    whole_before = shift(whole_before, "x", -1)
+    parts = [towards(0, 0), whole_across, whole_after, whole_before]
     node = node_call(parts, feats, vertex_rescaling_gain[None, :])
     mine = exchange(node.reshape(n_atoms, run, chans), ATOM_AXES)
 

time: 173 us -> 162 us (0.936)
  the two profiles are of different devices: /device:TPU:1 before, /device:TPU:8 now
where the time goes in v2:
time: 162 us; the launch traced here: 161 us
  Pallas kernels  56.4 us (35%)
  waiting for transfers between devices  43.7 us (27%)
  starting transfers between devices  41.4 us (26%)
  blocking collectives  16 us (10%)
  between operations  1.72 us (1%)
    ppermute x21, starting transfers between devices, shift(): lax.ppermute(value, axis, [(i, (i + by) % count) for i in range(count)])  27.6 us
    all_to_all x2, waiting for transfers between devices, exchange(): return lax.all_to_all(pieces, axes, 0, 0, tiled=True)  26.7 us
    ppermute x21, waiting for transfers between devices, shift(): lax.ppermute(value, axis, [(i, (i + by) % count) for i in range(count)])  17 us
    all_to_all x1, blocking collectives, exchange(): return lax.all_to_all(pieces, axes, 0, 0, tiled=True)  16 us
    pallas_call x1, Pallas kernels, struct_call(): pl.pallas_call(struct_kernel, out_shape=[jax.ShapeDtypeStruct(shape, BF)]...  14.3 us
    all_to_all x2, starting transfers between devices, exchange(): return lax.all_to_all(pieces, axes, 0, 0, tiled=True)  13.8 us
    pallas_call x8, Pallas kernels, update_call(): pl.pallas_call(update_kernel, out_shape=jax.ShapeDtypeStruct((TILE, chans...  12.8 us
    pallas_call x1, Pallas kernels, edges_call(): pl.pallas_call(edges_kernel, out_shape=jax.ShapeDtypeStruct((orb, edges),...  8.22 us
  transfers between devices with their start and end apart: 23, of which 9 were waited for; matrix products, arithmetic and copies ran while one was open for 0% of the time, Pallas kernels for 18%

profile of v2, /device:TPU:8, one launch (start us, length us, event | category | flops | bytes accessed | tf_op | source)
XLA Modules:
  0.0 161.4 jit_solution(7404966097115939275)
XLA Ops:
  0.7 14.3 %struct.1 = (bf16[16,2,16,256]{3,2,1,0:T(8,128)(2,1)S(1)}, bf16[16,2,16,256]{3,2,1,0:T(8,128)(2,1)S(1)}) custom-call(s32[1]{0:T(128)} %bitcast.3.core_ref, f32[3,4096]{1,0:T(4,128)} %coord_ref.3, f32[3,512]{1,0:T(4,128)} %kvec_ref.3, bf16[4096,256]{1,0:T(8,128)(2,1)} %feat_ref.3), custom_call_target="tpu_custom_call" | custom-call | flops 3221225472 | bytes 4194304 | tf_op jit(solution)/shard_map/struct/pallas_call | solution.py:119
  17.4 10.3 %all-to-all-start = ((bf16[16,2,16,256]{3,2,1,0:T(8,128)(2,1)}), bf16[16,2,16,256]{3,2,1,0:T(8,128)(2,1)S(1)}, u32[]{:S(2)}, u32[]{:S(2)}) async-start(bf16[16,2,16,256]{3,2,1,0:T(8,128)(2,1)} %add_convert_fusion), calls=%async_computation | async-start | bytes 524288 | tf_op jit(solution)/shard_map/all_to_all | solution.py:529
  27.7 13.7 %all-to-all-done = bf16[16,2,16,256]{3,2,1,0:T(8,128)(2,1)S(1)} async-done(((bf16[16,2,16,256]{3,2,1,0:T(8,128)(2,1)}), bf16[16,2,16,256]{3,2,1,0:T(8,128)(2,1)S(1)}, u32[]{:S(2)}, u32[]{:S(2)}) %all-to-all-start) | async-done | bytes 262176 | tf_op jit(solution)/shard_map/all_to_all | solution.py:529
  42.3 3.5 %all-to-all-start.1 = ((bf16[16,2,16,256]{3,2,1,0:T(8,128)(2,1)}), bf16[16,2,16,256]{3,2,1,0:T(8,128)(2,1)S(1)}, u32[]{:S(2)}, u32[]{:S(2)}) async-start(bf16[16,2,16,256]{3,2,1,0:T(8,128)(2,1)} %broadcast_in_dim.7), calls=%async_computation.1 | async-start | bytes 524288 | tf_op jit(solution)/shard_map/all_to_all | solution.py:529
  45.8 13.0 %all-to-all-done.1.own_ref = bf16[16,2,16,256]{3,2,1,0:T(8,128)(2,1)S(1)} async-done(((bf16[16,2,16,256]{3,2,1,0:T(8,128)(2,1)}), bf16[16,2,16,256]{3,2,1,0:T(8,128)(2,1)S(1)}, u32[]{:S(2)}, u32[]{:S(2)}) %all-to-all-start.1) | async-done | bytes 262176 | tf_op jit(solution)/shard_map/all_to_all | solution.py:529
  58.9 5.1 %order.1 = (bf16[4096,128]{1,0:T(8,128)(2,1)S(1)}, bf16[128,512]{1,0:T(8,128)(2,1)S(1)}) custom-call(s32[4096]{0:T(1024)S(1)} %fusion.11.place_ref, s32[1]{0:T(128)} %bitcast.3.core_ref, f32[3,4096]{1,0:T(4,128)S(1)} %copy-done.5, f32[3,512]{1,0:T(4,128)S(1)} %copy-done.6), custom_call_target="tpu_custom_call" | custom-call | flops 2147483648 | bytes 4194304 | tf_op jit(solution)/shard_map/order/pallas_call | solution.py:178
  64.0 1.6 update.13
  74.5 3.3 %collective-permute-start.8 = (bf16[256,256]{1,0:T(8,128)(2,1)S(1)}, bf16[256,256]{1,0:T(8,128)(2,1)S(1)}, u32[]{:S(2)}, u32[]{:S(2)}) collective-permute-start(bf16[256,256]{1,0:T(8,128)(2,1)S(1)} %get-tuple-element.18), channel_id=1, source_target_pairs={{0,3},{1,0},{2,1},{3,2},{4,7},{5,4},{6,5},{7,6},{8,11},{9,8},{10,9... | collective-permute-start | bytes 393224 | tf_op jit(solution)/shard_map/ppermute | solution.py:534
  77.8 1.6 update.14.refs_0_
  79.4 1.6 update.11.refs_0_
  84.2 3.3 %collective-permute-start.9 = (bf16[512,256]{1,0:T(8,128)(2,1)S(1)}, bf16[512,256]{1,0:T(8,128)(2,1)S(1)}, u32[]{:S(2)}, u32[]{:S(2)}) collective-permute-start(bf16[512,256]{1,0:T(8,128)(2,1)S(1)} %merge.7), channel_id=1, source_target_pairs={{0,3},{1,0},{2,1},{3,2},{4,7},{5,4},{6,5},{7,6},{8,11},{9,8},{10,9... | collective-permute-start | bytes 786440 | tf_op jit(solution)/shard_map/ppermute | solution.py:534
  88.3 5.7 %pick.1.refs_4_ = bf16[512,256]{1,0:T(8,128)(2,1)S(1)} custom-call(s32[1,4096]{1,0:T(1,128)S(1)} %fusion.20.want_ref, bf16[4096,256]{1,0:T(8,128)(2,1)} %feat_ref.3), custom_call_target="tpu_custom_call" | custom-call | flops 1073741824 | bytes 3145728 | tf_op jit(solution)/shard_map/pick/pallas_call | solution.py:223
  94.0 1.6 update.8.refs_0_
  96.2 16.0 %all_to_all.15.refs_0_ = bf16[32,16,256]{2,1,0:T(8,128)(2,1)S(1)} all-to-all(bf16[32,16,256]{2,1,0:T(8,128)(2,1)S(1)} %bitcast.7), channel_id=1, replica_groups=mesh['z'=8,'yh'=2,'core'=2,'yl'=2,'x'=4] {'z','yh','core'}, dimensions={0} | all-to-all | bytes 524288 | tf_op jit(solution)/shard_map/all_to_all | solution.py:529
  112.2 3.2 %collective-permute-start.10 = (bf16[32,16,256]{2,1,0:T(8,128)(2,1)S(1)}, bf16[32,16,256]{2,1,0:T(8,128)(2,1)S(1)}, u32[]{:S(2)}, u32[]{:S(2)}) collective-permute-start(bf16[32,16,256]{2,1,0:T(8,128)(2,1)S(1)} %all_to_all.15.refs_0_), channel_id=1, source_target_pairs={{0,3},{1,0},{2,1},{3,2},{4,7},{5,4},{6,5},{7,6},{8,11},{9,8},{10,9... | collective-permute-start | bytes 786440 | tf_op jit(solution)/shard_map/ppermute | solution.py:534
  116.1 5.9 %collective-permute-done.11.refs_4_ = bf16[32,16,256]{2,1,0:T(8,128)(2,1)S(1)} collective-permute-done((bf16[32,16,256]{2,1,0:T(8,128)(2,1)S(1)}, bf16[32,16,256]{2,1,0:T(8,128)(2,1)S(1)}, u32[]{:S(2)}, u32[]{:S(2)}) %collective-permute-start.11) | collective-permute-done | bytes 262176 | tf_op jit(solution)/shard_map/ppermute | solution.py:534
  122.1 3.3 %collective-permute-start.13 = (bf16[16,16,256]{2,1,0:T(8,128)(2,1)S(1)}, bf16[16,16,256]{2,1,0:T(8,128)(2,1)S(1)}, u32[]{:S(2)}, u32[]{:S(2)}) collective-permute-start(bf16[16,16,256]{2,1,0:T(8,128)(2,1)S(1)} %slice.9), channel_id=1, source_target_pairs={{0,3},{1,0},{2,1},{3,2},{4,7},{5,4},{6,5},{7,6},{8,11},{9,8},{10,9... | collective-permute-start | bytes 393224 | tf_op jit(solution)/shard_map/ppermute | solution.py:534
  126.1 2.2 %collective-permute-done.12.refs_2_ = bf16[16,16,256]{2,1,0:T(8,128)(2,1)S(1)} collective-permute-done((bf16[16,16,256]{2,1,0:T(8,128)(2,1)S(1)}, bf16[16,16,256]{2,1,0:T(8,128)(2,1)S(1)}, u32[]{:S(2)}, u32[]{:S(2)}) %collective-permute-start.12) | collective-permute-done | bytes 131104 | tf_op jit(solution)/shard_map/ppermute | solution.py:534
  131.0 3.6 %collective-permute-done.15.refs_6_ = bf16[32,16,256]{2,1,0:T(8,128)(2,1)S(1)} collective-permute-done((bf16[32,16,256]{2,1,0:T(8,128)(2,1)S(1)}, bf16[32,16,256]{2,1,0:T(8,128)(2,1)S(1)}, u32[]{:S(2)}, u32[]{:S(2)}) %collective-permute-start.15) | collective-permute-done | bytes 262176 | tf_op jit(solution)/shard_map/ppermute | solution.py:534
  134.6 2.2 %collective-permute-done.16.refs_7_ = bf16[16,16,256]{2,1,0:T(8,128)(2,1)S(1)} collective-permute-done((bf16[16,16,256]{2,1,0:T(8,128)(2,1)S(1)}, bf16[16,16,256]{2,1,0:T(8,128)(2,1)S(1)}, u32[]{:S(2)}, u32[]{:S(2)}) %collective-permute-start.16) | collective-permute-done | bytes 131104 | tf_op jit(solution)/shard_map/ppermute | solution.py:534
  138.2 2.5 %halo.1 = (f32[8192,128]{1,0:T(8,128)S(1)}, bf16[512,256]{1,0:T(8,128)(2,1)S(1)}, bf16[512,256]{1,0:T(8,128)(2,1)S(1)}) custom-call(s32[8]{0:T(128)S(1)} %fusion.27.kv_ref, s32[1024]{0:T(1024)S(1)} %add_multiply_fusion.ids_ref, bf16[32,16,256]{2,1,0:T(8,128)(2,1)S(1)} %all_to_all.15.refs_0_, bf16[32,16,256]{2,1,0:T(8,128)(2,1)S(1)} %collective-permute-done.10.refs_1_, ...), custom_call_target="tpu_custom_call" | custom-call | flops 536870912 | bytes 8388608 | tf_op jit(solution)/shard_map/halo/pallas_call | solution.py:395
  140.8 5.3 %collective-permute-start.20 = (bf16[512,256]{1,0:T(8,128)(2,1)S(1)}, bf16[512,256]{1,0:T(8,128)(2,1)S(1)}, u32[]{:S(2)}, u32[]{:S(2)}) collective-permute-start(bf16[512,256]{1,0:T(8,128)(2,1)S(1)} %get-tuple-element.21), channel_id=1, source_target_pairs={{0,248},{8,0},{16,8},{24,16},{32,24},{40,32},{48,40},{56,48},{64,5... | collective-permute-start | bytes 786440 | tf_op jit(solution)/shard_map/ppermute | solution.py:534
  146.2 7.0 %right.1 = (bf16[32,8,16,256]{3,2,1,0:T(8,128)(2,1)}, f32[8192,128]{1,0:T(8,128)S(1)}) custom-call(s32[8]{0:T(128)S(1)} %fusion.27.kv_ref, s32[4096]{0:T(1024)S(1)} %broadcast_multiply_fusion.dst_ref, bf16[32,16,256]{2,1,0:T(8,128)(2,1)S(1)} %all_to_all.15.refs_0_, bf16[32,16,256]{2,1,0:T(8,128)(2,1)S(1)} %collective-permute-done.10.refs_1_, ...), custom_call_target="tpu_custom_call" | custom-call | flops 536870912 | bytes 8388608 | tf_op jit(solution)/shard_map/right/pallas_call | solution.py:442
  153.2 8.2 %edges.1 = bf16[196,4096]{1,0:T(8,128)(2,1)} custom-call(s32[4096]{0:T(1024)S(1)} %broadcast_multiply_fusion.1.src_ref, s32[1]{0:T(128)S(6)} %copy.16.count_ref, f32[8192,128]{1,0:T(8,128)S(1)} %get-tuple-element.19.left_ref, bf16[512,256]{1,0:T(8,128)(2,1)S(1)} %collective-permute-done.19.lower_ref, bf16[512,256]{1,0:T(8,128)(2,1)S(1)} %collective-permute-done.20.upper_ref, ...), custom_call_target="tpu_custom_call" | custom-call | flops 411041792 | bytes 8388608 | tf_op jit(solution)/shard_map/edges/pallas_call | solution.py:503
  (79 shorter events, 21.6 us)
Async XLA Ops:
  15.0 1.6 %collective-permute-start = (bf16[16,2,16,256]{3,2,1,0:T(8,128)(2,1)S(1)}, bf16[16,2,16,256]{3,2,1,0:T(8,128)(2,1)S(1)}, u32[]{:S(2)}, u32[]{:S(2)}) collective-permute-start(bf16[16,2,16,256]{3,2,1,0:T(8,128)(2,1)S(1)} %get-tuple-element.16), channel_id=1, source_target_pairs={{0,8},{8,0},{1,9},{9,1},{2,10},{10,2},{3,11},{11,3},{4,12},{12,4},... | collective-permute-start | bytes 786440 | tf_op jit(solution)/shard_map/ppermute | solution.py:534
  17.4 24.1 %all-to-all-start = ((bf16[16,2,16,256]{3,2,1,0:T(8,128)(2,1)}), bf16[16,2,16,256]{3,2,1,0:T(8,128)(2,1)S(1)}, u32[]{:S(2)}, u32[]{:S(2)}) async-start(bf16[16,2,16,256]{3,2,1,0:T(8,128)(2,1)} %add_convert_fusion), calls=%async_computation | async-start | bytes 524288 | tf_op jit(solution)/shard_map/all_to_all | solution.py:529
  42.3 16.5 %all-to-all-start.1 = ((bf16[16,2,16,256]{3,2,1,0:T(8,128)(2,1)}), bf16[16,2,16,256]{3,2,1,0:T(8,128)(2,1)S(1)}, u32[]{:S(2)}, u32[]{:S(2)}) async-start(bf16[16,2,16,256]{3,2,1,0:T(8,128)(2,1)} %broadcast_in_dim.7), calls=%async_computation.1 | async-start | bytes 524288 | tf_op jit(solution)/shard_map/all_to_all | solution.py:529
  58.8 5.2 %collective-permute-start.1 = (bf16[16,2,16,256]{3,2,1,0:T(8,128)(2,1)S(1)}, bf16[16,2,16,256]{3,2,1,0:T(8,128)(2,1)S(1)}, u32[]{:S(2)}, u32[]{:S(2)}) collective-permute-start(bf16[16,2,16,256]{3,2,1,0:T(8,128)(2,1)S(1)} %all-to-all-done.1.own_ref), channel_id=1, source_target_pairs={{0,8},{8,0},{1,9},{9,1},{2,10},{10,2},{3,11},{11,3},{4,12},{12,4},... | collective-permute-start | bytes 786440 | tf_op jit(solution)/shard_map/ppermute | solution.py:534
  65.6 8.8 %collective-permute-start.4 = (bf16[512,256]{1,0:T(8,128)(2,1)S(1)}, bf16[512,256]{1,0:T(8,128)(2,1)S(1)}, u32[]{:S(2)}, u32[]{:S(2)}) collective-permute-start(bf16[512,256]{1,0:T(8,128)(2,1)S(1)} %update.13), channel_id=1, source_target_pairs={{0,4},{4,0},{1,5},{5,1},{2,6},{6,2},{3,7},{7,3},{8,12},{12,8},{9,1... | collective-permute-start | bytes 786440 | tf_op jit(solution)/shard_map/ppermute | solution.py:534
  68.7 13.9 %collective-permute-start.2 = (bf16[512,256]{1,0:T(8,128)(2,1)S(1)}, bf16[512,256]{1,0:T(8,128)(2,1)S(1)}, u32[]{:S(2)}, u32[]{:S(2)}) collective-permute-start(bf16[512,256]{1,0:T(8,128)(2,1)S(1)} %update.10), channel_id=1, source_target_pairs={{0,1},{1,2},{2,3},{3,0},{4,5},{5,6},{6,7},{7,4},{8,9},{9,10},{10,1... | collective-permute-start | bytes 786440 | tf_op jit(solution)/shard_map/ppermute | solution.py:534
  71.8 12.3 %collective-permute-start.7 = (bf16[512,256]{1,0:T(8,128)(2,1)S(1)}, bf16[512,256]{1,0:T(8,128)(2,1)S(1)}, u32[]{:S(2)}, u32[]{:S(2)}) collective-permute-start(bf16[512,256]{1,0:T(8,128)(2,1)S(1)} %update.15), channel_id=1, source_target_pairs={{0,4},{4,0},{1,5},{5,1},{2,6},{6,2},{3,7},{7,3},{8,12},{12,8},{9,1... | collective-permute-start | bytes 786440 | tf_op jit(solution)/shard_map/ppermute | solution.py:534
  74.5 9.6 %collective-permute-start.8 = (bf16[256,256]{1,0:T(8,128)(2,1)S(1)}, bf16[256,256]{1,0:T(8,128)(2,1)S(1)}, u32[]{:S(2)}, u32[]{:S(2)}) collective-permute-start(bf16[256,256]{1,0:T(8,128)(2,1)S(1)} %get-tuple-element.18), channel_id=1, source_target_pairs={{0,3},{1,0},{2,1},{3,2},{4,7},{5,4},{6,5},{7,6},{8,11},{9,8},{10,9... | collective-permute-start | bytes 393224 | tf_op jit(solution)/shard_map/ppermute | solution.py:534
  77.8 9.7 %collective-permute-start.5 = (bf16[256,256]{1,0:T(8,128)(2,1)S(1)}, bf16[256,256]{1,0:T(8,128)(2,1)S(1)}, u32[]{:S(2)}, u32[]{:S(2)}) collective-permute-start(bf16[256,256]{1,0:T(8,128)(2,1)S(1)} %get-tuple-element.17), channel_id=1, source_target_pairs={{0,1},{1,2},{2,3},{3,0},{4,5},{5,6},{6,7},{7,4},{8,9},{9,10},{10,1... | collective-permute-start | bytes 393224 | tf_op jit(solution)/shard_map/ppermute | solution.py:534
  82.7 12.9 %collective-permute-start.3 = (bf16[512,256]{1,0:T(8,128)(2,1)S(1)}, bf16[512,256]{1,0:T(8,128)(2,1)S(1)}, u32[]{:S(2)}, u32[]{:S(2)}) collective-permute-start(bf16[512,256]{1,0:T(8,128)(2,1)S(1)} %merge.4), channel_id=1, source_target_pairs={{0,4},{4,0},{1,5},{5,1},{2,6},{6,2},{3,7},{7,3},{8,12},{12,8},{9,1... | collective-permute-start | bytes 786440 | tf_op jit(solution)/shard_map/ppermute | solution.py:534
  84.2 11.4 %collective-permute-start.9 = (bf16[512,256]{1,0:T(8,128)(2,1)S(1)}, bf16[512,256]{1,0:T(8,128)(2,1)S(1)}, u32[]{:S(2)}, u32[]{:S(2)}) collective-permute-start(bf16[512,256]{1,0:T(8,128)(2,1)S(1)} %merge.7), channel_id=1, source_target_pairs={{0,3},{1,0},{2,1},{3,2},{4,7},{5,4},{6,5},{7,6},{8,11},{9,8},{10,9... | collective-permute-start | bytes 786440 | tf_op jit(solution)/shard_map/ppermute | solution.py:534
  87.6 8.1 %collective-permute-start.6 = (bf16[512,256]{1,0:T(8,128)(2,1)S(1)}, bf16[512,256]{1,0:T(8,128)(2,1)S(1)}, u32[]{:S(2)}, u32[]{:S(2)}) collective-permute-start(bf16[512,256]{1,0:T(8,128)(2,1)S(1)} %merge.6), channel_id=1, source_target_pairs={{0,1},{1,2},{2,3},{3,0},{4,5},{5,6},{6,7},{7,4},{8,9},{9,10},{10,1... | collective-permute-start | bytes 786440 | tf_op jit(solution)/shard_map/ppermute | solution.py:534
  95.6 50.5 %copy-start.9 = (s32[4096]{0:T(1024)S(1)}, s32[4096]{0:T(1024)}, u32[]{:S(2)}) copy-start(s32[4096]{0:T(1024)} %param.25) | copy-start | bytes 49156
  112.2 9.8 %collective-permute-start.11 = (bf16[32,16,256]{2,1,0:T(8,128)(2,1)S(1)}, bf16[32,16,256]{2,1,0:T(8,128)(2,1)S(1)}, u32[]{:S(2)}, u32[]{:S(2)}) collective-permute-start(bf16[32,16,256]{2,1,0:T(8,128)(2,1)S(1)} %all_to_all.15.refs_0_), channel_id=1, source_target_pairs={{0,1},{1,2},{2,3},{3,0},{4,5},{5,6},{6,7},{7,4},{8,9},{9,10},{10,1... | collective-permute-start | bytes 786440 | tf_op jit(solution)/shard_map/ppermute | solution.py:534
  112.2 9.9 %collective-permute-start.10 = (bf16[32,16,256]{2,1,0:T(8,128)(2,1)S(1)}, bf16[32,16,256]{2,1,0:T(8,128)(2,1)S(1)}, u32[]{:S(2)}, u32[]{:S(2)}) collective-permute-start(bf16[32,16,256]{2,1,0:T(8,128)(2,1)S(1)} %all_to_all.15.refs_0_), channel_id=1, source_target_pairs={{0,3},{1,0},{2,1},{3,2},{4,7},{5,4},{6,5},{7,6},{8,11},{9,8},{10,9... | collective-permute-start | bytes 786440 | tf_op jit(solution)/shard_map/ppermute | solution.py:534
  115.4 10.7 %collective-permute-start.14 = (bf16[32,16,256]{2,1,0:T(8,128)(2,1)S(1)}, bf16[32,16,256]{2,1,0:T(8,128)(2,1)S(1)}, u32[]{:S(2)}, u32[]{:S(2)}) collective-permute-start(bf16[32,16,256]{2,1,0:T(8,128)(2,1)S(1)} %all_to_all.15.refs_0_), channel_id=1, source_target_pairs={{0,4},{4,0},{1,5},{5,1},{2,6},{6,2},{3,7},{7,3},{8,12},{12,8},{9,1... | collective-permute-start | bytes 786440 | tf_op jit(solution)/shard_map/ppermute | solution.py:534
  122.0 6.3 %collective-permute-start.12 = (bf16[16,16,256]{2,1,0:T(8,128)(2,1)S(1)}, bf16[16,16,256]{2,1,0:T(8,128)(2,1)S(1)}, u32[]{:S(2)}, u32[]{:S(2)}) collective-permute-start(bf16[16,16,256]{2,1,0:T(8,128)(2,1)S(1)} %slice.8), channel_id=1, source_target_pairs={{0,1},{1,2},{2,3},{3,0},{4,5},{5,6},{6,7},{7,4},{8,9},{9,10},{10,1... | collective-permute-start | bytes 393224 | tf_op jit(solution)/shard_map/ppermute | solution.py:534
  122.1 6.8 %collective-permute-start.13 = (bf16[16,16,256]{2,1,0:T(8,128)(2,1)S(1)}, bf16[16,16,256]{2,1,0:T(8,128)(2,1)S(1)}, u32[]{:S(2)}, u32[]{:S(2)}) collective-permute-start(bf16[16,16,256]{2,1,0:T(8,128)(2,1)S(1)} %slice.9), channel_id=1, source_target_pairs={{0,3},{1,0},{2,1},{3,2},{4,7},{5,4},{6,5},{7,6},{8,11},{9,8},{10,9... | collective-permute-start | bytes 393224 | tf_op jit(solution)/shard_map/ppermute | solution.py:534
  125.4 9.2 %collective-permute-start.15 = (bf16[32,16,256]{2,1,0:T(8,128)(2,1)S(1)}, bf16[32,16,256]{2,1,0:T(8,128)(2,1)S(1)}, u32[]{:S(2)}, u32[]{:S(2)}) collective-permute-start(bf16[32,16,256]{2,1,0:T(8,128)(2,1)S(1)} %collective-permute-done.10.refs_1_), channel_id=1, source_target_pairs={{0,4},{4,0},{1,5},{5,1},{2,6},{6,2},{3,7},{7,3},{8,12},{12,8},{9,1... | collective-permute-start | bytes 786440 | tf_op jit(solution)/shard_map/ppermute | solution.py:534
  126.1 8.5 %collective-permute-start.18 = (bf16[32,16,256]{2,1,0:T(8,128)(2,1)S(1)}, bf16[32,16,256]{2,1,0:T(8,128)(2,1)S(1)}, u32[]{:S(2)}, u32[]{:S(2)}) collective-permute-start(bf16[32,16,256]{2,1,0:T(8,128)(2,1)S(1)} %collective-permute-done.14.refs_5_), channel_id=1, source_target_pairs={{0,1},{1,2},{2,3},{3,0},{4,5},{5,6},{6,7},{7,4},{8,9},{9,10},{10,1... | collective-permute-start | bytes 786440 | tf_op jit(solution)/shard_map/ppermute | solution.py:534
  128.3 8.5 %collective-permute-start.16 = (bf16[16,16,256]{2,1,0:T(8,128)(2,1)S(1)}, bf16[16,16,256]{2,1,0:T(8,128)(2,1)S(1)}, u32[]{:S(2)}, u32[]{:S(2)}) collective-permute-start(bf16[16,16,256]{2,1,0:T(8,128)(2,1)S(1)} %collective-permute-done.12.refs_2_), channel_id=1, source_target_pairs={{0,4},{4,0},{1,5},{5,1},{2,6},{6,2},{3,7},{7,3},{8,12},{12,8},{9,1... | collective-permute-start | bytes 393224 | tf_op jit(solution)/shard_map/ppermute | solution.py:534
  128.9 9.3 %collective-permute-start.17 = (bf16[16,16,256]{2,1,0:T(8,128)(2,1)S(1)}, bf16[16,16,256]{2,1,0:T(8,128)(2,1)S(1)}, u32[]{:S(2)}, u32[]{:S(2)}) collective-permute-start(bf16[16,16,256]{2,1,0:T(8,128)(2,1)S(1)} %collective-permute-done.13.refs_3_), channel_id=1, source_target_pairs={{0,4},{4,0},{1,5},{5,1},{2,6},{6,2},{3,7},{7,3},{8,12},{12,8},{9,1... | collective-permute-start | bytes 393224 | tf_op jit(solution)/shard_map/ppermute | solution.py:534
  140.7 12.5 %collective-permute-start.19 = (bf16[512,256]{1,0:T(8,128)(2,1)S(1)}, bf16[512,256]{1,0:T(8,128)(2,1)S(1)}, u32[]{:S(2)}, u32[]{:S(2)}) collective-permute-start(bf16[512,256]{1,0:T(8,128)(2,1)S(1)} %get-tuple-element.20), channel_id=1, source_target_pairs={{0,8},{8,16},{16,24},{24,32},{32,40},{40,48},{48,56},{56,64},{64,7... | collective-permute-start | bytes 786440 | tf_op jit(solution)/shard_map/ppermute | solution.py:534
  140.8 12.4 %collective-permute-start.20 = (bf16[512,256]{1,0:T(8,128)(2,1)S(1)}, bf16[512,256]{1,0:T(8,128)(2,1)S(1)}, u32[]{:S(2)}, u32[]{:S(2)}) collective-permute-start(bf16[512,256]{1,0:T(8,128)(2,1)S(1)} %get-tuple-element.21), channel_id=1, source_target_pairs={{0,248},{8,0},{16,8},{24,16},{32,24},{40,32},{48,40},{56,48},{64,5... | collective-permute-start | bytes 786440 | tf_op jit(solution)/shard_map/ppermute | solution.py:534
  (11 other events, 389.1 us)
